TPU v7x, 32 devices: a whole 2x2x4 slice. The times are simulated.
32 devices in a mesh: ctx: 8 (over y, x, core), wt: 4 (over z).
Axes of the slice: x: 2, y: 2, z: 4, core: 2. Of those that a mesh axis runs over, the one named last changes fastest.
Arguments:
- tokens: bfloat16 [2, 4, 1024, 768], P(None, 'wt', 'ctx'), may hold values from -6 to 6
- doc_lengths: int32 [2, 4, 16], P(None, 'wt'), may hold values from 1 to 512, 1024 in all within a row
- query_weight: bfloat16 [768, 768], P('wt'), may hold values from -0.3125 to 0.3125
- query_bias: bfloat16 [768], P('wt'), may hold values from -1.5 to 1.5
- key_weight: bfloat16 [768, 768], P('wt'), may hold values from -0.3125 to 0.3125
- value_weight: bfloat16 [768, 768], P('wt'), may hold values from -0.21875 to 0.21875
- value_bias: bfloat16 [768], P('wt'), may hold values from -1.5 to 1.5
- out_weight: bfloat16 [768, 768], P('wt'), may hold values from -1.25 to 1.25
- out_bias: bfloat16 [768], P('wt'), may hold values from -1.5 to 1.5
- first_gain: bfloat16 [768], P('wt'), may hold values from 0.5 to 1.5
- first_shift: bfloat16 [768], P('wt'), may hold values from -1.5 to 1.5
- inner_weight: bfloat16 [768, 3072], P('wt'), may hold values from -0.21875 to 0.21875
- inner_bias: bfloat16 [3072], P('wt'), may hold values from -1.5 to 1.5
- outer_weight: bfloat16 [3072, 768], P('wt'), may hold values from -0.109375 to 0.109375
- outer_bias: bfloat16 [768], P('wt'), may hold values from -1.5 to 1.5
- second_gain: bfloat16 [768], P('wt'), may hold values from 0.5 to 1.5
- second_shift: bfloat16 [768], P('wt'), may hold values from -1.5 to 1.5
- cotangent: bfloat16 [2, 4, 1024, 768], P(None, 'wt', 'ctx'), may hold values from -6 to 6
Outputs:
- block_output: bfloat16 [2, 4, 1024, 768], P(None, 'wt', 'ctx')
- tokens_gradient: float32 [2, 4, 1024, 768], P(None, 'wt', 'ctx')
- query_weight_gradient: float32 [768, 768], P('wt')
- query_bias_gradient: float32 [768], P('wt')
- key_weight_gradient: float32 [768, 768], P('wt')
- value_weight_gradient: float32 [768, 768], P('wt')
- value_bias_gradient: float32 [768], P('wt')
- out_weight_gradient: float32 [768, 768], P('wt')
- out_bias_gradient: float32 [768], P('wt')
- first_gain_gradient: float32 [768], P('wt')
- first_shift_gradient: float32 [768], P('wt')
- inner_weight_gradient: float32 [768, 3072], P('wt')
- inner_bias_gradient: float32 [3072], P('wt')
- outer_weight_gradient: float32 [3072, 768], P('wt')
- outer_bias_gradient: float32 [768], P('wt')
- second_gain_gradient: float32 [768], P('wt')
- second_shift_gradient: float32 [768], P('wt')
Inputs may be any that keep to these rules, and one draw needn't show every extreme that they name: `doc_lengths`: each row holds the lengths of the 16 documents of one packed sequence in order; a row sums to 1024 and its longest document has exactly 512 tokens.
All inputs are finite; a program needn't handle non-finite values.
Results may differ from a plain program's by a relative error of at most 0.02.
Values may be sent and summed in bfloat16 or wider, within the bound.
No kernel may reach another device: no remote copies, remote signals or barrier semaphores. Data moves between devices by JAX's collectives and lax.ppermute only.
A program may use at most 256 MiB of HBM per device.

v0:
```python
import math

import jax
import jax.numpy as jnp
from jax import lax
from jax.sharding import PartitionSpec as P

HEADS = 12
HEAD_DIM = 64


EPS = 1e-12
NEG = -1e30
ROOT_HALF = 0.7071067811865476


def for_sending(shard):

    def short(part):
        return part.astype(jnp.bfloat16) if part.dtype == jnp.float32 else part

    return jax.tree.map(short, shard)


def normalize(rows, gain, shift):
    mean = jnp.mean(rows, axis=-1, keepdims=True)
    centered = rows - mean
    spread = jnp.mean(centered * centered, axis=-1, keepdims=True)
    return centered * lax.rsqrt(spread + EPS) * gain + shift


def gelu(inner):
    return 0.5 * inner * (1.0 + lax.erf(inner * ROOT_HALF))


def segment_of(starts, positions):
    found = (starts[:, None, :] <= positions[:, :, None]).astype(jnp.int32)
    return jnp.sum(found, axis=-1) - 1


def project(inputs, weight):
    return jnp.einsum("btd,de->bte", inputs, weight, preferred_element_type=jnp.float32)


def project_back(grads, weight):
    return jnp.einsum("bte,de->btd", grads, weight, preferred_element_type=jnp.float32)


def outer_sum(inputs, grads):
    return jnp.einsum("btd,bte->de", inputs, grads, preferred_element_type=jnp.float32)


def row_sum(grads):
    return jnp.sum(grads.astype(jnp.float32), axis=(0, 1))


def heads_of(array):
    return array.reshape(array.shape[0], array.shape[1], HEADS, HEAD_DIM)


def block_loop(width, carry, visit):
    block = math.gcd(width, 512)

    def step(state, index):
        return (visit(state, index * block, block), None)

    carry, unused = lax.scan(step, carry, jnp.arange(width // block, dtype=jnp.int32))
    return carry


def reaches(starts, own_seg, first, count):
    positions = first + jnp.arange(count, dtype=jnp.int32)
    other = segment_of(starts, jnp.broadcast_to(positions, (starts.shape[0], count)))
    touch = jnp.any((other[:, 0] <= own_seg[:, -1]) & (other[:, -1] >= own_seg[:, 0]))
    return (other, touch)


def keep_state(state):
    return state


def forward_attention(queries, query_seg, starts, keys, values):
    scale = HEAD_DIM ** (-0.5)
    batch, rows = (queries.shape[0], queries.shape[1])
    query_heads = heads_of(queries)

    def forward_fold(carry, piece, start):
        key_piece, value_piece = piece

        def visit(state, offset, count):
            other, touch = reaches(starts, query_seg, offset, count)

            def compute(state):
                top, total, accum = state
                key_block = heads_of(lax.dynamic_slice_in_dim(key_piece, offset, count, 1))
                value_block = heads_of(lax.dynamic_slice_in_dim(value_piece, offset, count, 1))
                scores = (
                    jnp.einsum(
                        "bqhd,bkhd->bhqk",
                        query_heads,
                        key_block,
                        preferred_element_type=jnp.float32,
                    )
                    * scale
                )
                mask = (query_seg[:, :, None] == other[:, None, :])[:, None]
                scores = jnp.where(mask, scores, NEG)
                new_top = jnp.maximum(top, jnp.max(scores, axis=-1))
                expd = jnp.where(mask, jnp.exp(scores - new_top[..., None]), 0.0)
                factor = jnp.exp(top - new_top)
                total = total * factor + jnp.sum(expd, axis=-1)
                added = jnp.einsum(
                    "bhqk,bkhd->bqhd",
                    expd.astype(jnp.bfloat16),
                    value_block,
                    preferred_element_type=jnp.float32,
                )
                accum = accum * jnp.transpose(factor, (0, 2, 1))[..., None] + added
                return (new_top, total, accum)

            return lax.cond(touch, compute, keep_state, state)

        return block_loop(key_piece.shape[1], carry, visit)

    init = (
        jnp.full((batch, HEADS, rows), NEG, jnp.float32),
        jnp.zeros((batch, HEADS, rows), jnp.float32),
        jnp.zeros((batch, rows, HEADS, HEAD_DIM), jnp.float32),
    )
    whole = (keys, values)
    top, total, accum = forward_fold(
        init,
        (
            lax.all_gather(keys, "ctx", axis=1, tiled=True),
            lax.all_gather(values, "ctx", axis=1, tiled=True),
        ),
        jnp.int32(0),
    )
    mixed = accum / jnp.transpose(total, (0, 2, 1))[..., None]
    return (mixed, top + jnp.log(total), whole)


def query_gradient(queries, query_seg, starts, keys, values, dmixed, logsum, delta):
    scale = HEAD_DIM ** (-0.5)
    query_heads = heads_of(queries)
    grad_heads = heads_of(dmixed)

    def query_fold(carry, piece, start):
        key_piece, value_piece = piece

        def visit(state, offset, count):
            other, touch = reaches(starts, query_seg, offset, count)

            def compute(state):
                key_block = heads_of(lax.dynamic_slice_in_dim(key_piece, offset, count, 1))
                value_block = heads_of(lax.dynamic_slice_in_dim(value_piece, offset, count, 1))
                scores = (
                    jnp.einsum(
                        "bqhd,bkhd->bhqk",
                        query_heads,
                        key_block,
                        preferred_element_type=jnp.float32,
                    )
                    * scale
                )
                mask = (query_seg[:, :, None] == other[:, None, :])[:, None]
                probs = jnp.where(
                    mask, jnp.exp(jnp.where(mask, scores, NEG) - logsum[..., None]), 0.0
                )
                dprobs = jnp.einsum(
                    "bqhd,bkhd->bhqk", grad_heads, value_block, preferred_element_type=jnp.float32
                )
                dscores = (probs * (dprobs - delta[..., None])).astype(jnp.bfloat16)
                return (
                    state
                    + jnp.einsum(
                        "bhqk,bkhd->bqhd", dscores, key_block, preferred_element_type=jnp.float32
                    )
                    * scale
                )

            return lax.cond(touch, compute, keep_state, state)

        return block_loop(key_piece.shape[1], carry, visit)

    init = jnp.zeros(query_heads.shape, jnp.float32)
    return query_fold(
        init,
        (
            lax.all_gather(keys, "ctx", axis=1, tiled=True),
            lax.all_gather(values, "ctx", axis=1, tiled=True),
        ),
        jnp.int32(0),
    )


def key_gradient(keys, values, key_seg, starts, queries, dmixed, logsum, delta):
    scale = HEAD_DIM ** (-0.5)
    key_heads = heads_of(keys)
    value_heads = heads_of(values)
    every_top, every_delta = (
        lax.all_gather(logsum, "ctx", axis=2, tiled=True),
        lax.all_gather(delta, "ctx", axis=2, tiled=True),
    )

    def key_fold(carry, piece, start):
        query_piece, grad_piece = piece

        def visit(state, offset, count):
            other, touch = reaches(starts, key_seg, offset, count)

            def compute(state):
                dkeys, dvalues = state
                query_block = heads_of(lax.dynamic_slice_in_dim(query_piece, offset, count, 1))
                grad_block = heads_of(lax.dynamic_slice_in_dim(grad_piece, offset, count, 1))
                top_block = lax.dynamic_slice_in_dim(every_top, offset, count, 2)
                delta_block = lax.dynamic_slice_in_dim(every_delta, offset, count, 2)
                scores = (
                    jnp.einsum(
                        "bqhd,bkhd->bhqk",
                        query_block,
                        key_heads,
                        preferred_element_type=jnp.float32,
                    )
                    * scale
                )
                mask = (other[:, :, None] == key_seg[:, None, :])[:, None]
                probs = jnp.where(
                    mask, jnp.exp(jnp.where(mask, scores, NEG) - top_block[..., None]), 0.0
                )
                dvalues = dvalues + jnp.einsum(
                    "bhqk,bqhd->bkhd",
                    probs.astype(jnp.bfloat16),
                    grad_block,
                    preferred_element_type=jnp.float32,
                )
                dprobs = jnp.einsum(
                    "bqhd,bkhd->bhqk", grad_block, value_heads, preferred_element_type=jnp.float32
                )
                dscores = (probs * (dprobs - delta_block[..., None])).astype(jnp.bfloat16)
                dkeys = (
                    dkeys
                    + jnp.einsum(
                        "bhqk,bqhd->bkhd", dscores, query_block, preferred_element_type=jnp.float32
                    )
                    * scale
                )
                return (dkeys, dvalues)

            return lax.cond(touch, compute, keep_state, state)

        return block_loop(query_piece.shape[1], carry, visit)

    empty = jnp.zeros(key_heads.shape, jnp.float32)
    return key_fold(
        (empty, empty),
        (
            lax.all_gather(queries, "ctx", axis=1, tiled=True),
            lax.all_gather(dmixed, "ctx", axis=1, tiled=True),
        ),
        jnp.int32(0),
    )


def forward_pass(tokens, starts, weights, base):
    (
        query_weight,
        query_bias,
        key_weight,
        value_weight,
        value_bias,
        out_weight,
        out_bias,
        first_gain,
        first_shift,
        inner_weight,
        inner_bias,
        outer_weight,
        outer_bias,
        second_gain,
        second_shift,
    ) = weights
    rows = tokens.shape[1]
    positions = base + jnp.arange(rows, dtype=jnp.int32)
    query_seg = segment_of(starts, jnp.broadcast_to(positions, (tokens.shape[0], rows)))
    queries = (project(tokens, query_weight) + query_bias.astype(jnp.float32)).astype(jnp.bfloat16)
    keys = project(tokens, key_weight).astype(jnp.bfloat16)
    values = (project(tokens, value_weight) + value_bias.astype(jnp.float32)).astype(jnp.bfloat16)
    mixed, logsum, whole = forward_attention(queries, query_seg, starts, keys, values)
    mixed_low = mixed.reshape(tokens.shape).astype(jnp.bfloat16)
    first_sum = (
        tokens.astype(jnp.float32) + project(mixed_low, out_weight) + out_bias.astype(jnp.float32)
    )
    first = normalize(first_sum, first_gain.astype(jnp.float32), first_shift.astype(jnp.float32))
    first_low = first.astype(jnp.bfloat16)
    inner = project(first_low, inner_weight) + inner_bias.astype(jnp.float32)
    active = gelu(inner).astype(jnp.bfloat16)
    second_sum = first + project(active, outer_weight) + outer_bias.astype(jnp.float32)
    output = normalize(
        second_sum, second_gain.astype(jnp.float32), second_shift.astype(jnp.float32)
    ).astype(jnp.bfloat16)
    saved = (
        tokens,
        query_seg,
        queries,
        keys,
        values,
        mixed,
        logsum,
        mixed_low,
        first_sum,
        first_low,
        inner,
        active,
        second_sum,
        whole,
    )
    return (output, saved)


def backward_pass(saved, starts, weights, cotangent):
    (
        query_weight,
        query_bias,
        key_weight,
        value_weight,
        value_bias,
        out_weight,
        out_bias,
        first_gain,
        first_shift,
        inner_weight,
        inner_bias,
        outer_weight,
        outer_bias,
        second_gain,
        second_shift,
    ) = weights
    (
        tokens,
        query_seg,
        queries,
        keys,
        values,
        mixed,
        logsum,
        mixed_low,
        first_sum,
        first_low,
        inner,
        active,
        second_sum,
        whole,
    ) = saved
    unused, second_back = jax.vjp(
        normalize, second_sum, second_gain.astype(jnp.float32), second_shift.astype(jnp.float32)
    )
    dsecond, dgain_second, dshift_second = second_back(cotangent.astype(jnp.float32))
    douter = dsecond.astype(jnp.bfloat16)
    dactive = project_back(douter, outer_weight)
    unused, gelu_back = jax.vjp(gelu, inner)
    dinner = gelu_back(dactive)[0].astype(jnp.bfloat16)
    dfirst = dsecond + project_back(dinner, inner_weight)
    unused, first_back = jax.vjp(
        normalize, first_sum, first_gain.astype(jnp.float32), first_shift.astype(jnp.float32)
    )
    dfirst_sum, dgain_first, dshift_first = first_back(dfirst)
    dbranch = dfirst_sum.astype(jnp.bfloat16)
    dmixed = project_back(dbranch, out_weight).astype(jnp.bfloat16)
    delta = jnp.einsum("bqhd,bqhd->bhq", heads_of(dmixed).astype(jnp.float32), mixed)
    dqueries = query_gradient(queries, query_seg, starts, keys, values, dmixed, logsum, delta)
    dkeys, dvalues = key_gradient(keys, values, query_seg, starts, queries, dmixed, logsum, delta)
    dqueries = dqueries.reshape(tokens.shape).astype(jnp.bfloat16)
    dkeys = dkeys.reshape(tokens.shape).astype(jnp.bfloat16)
    dvalues = dvalues.reshape(tokens.shape).astype(jnp.bfloat16)
    tokens_grad = (
        dfirst_sum
        + project_back(dqueries, query_weight)
        + project_back(dkeys, key_weight)
        + project_back(dvalues, value_weight)
    )
    sums = (
        outer_sum(tokens, dqueries),
        row_sum(dqueries),
        outer_sum(tokens, dkeys),
        outer_sum(tokens, dvalues),
        row_sum(dvalues),
        outer_sum(mixed_low, dbranch),
        row_sum(dbranch),
        dgain_first,
        dshift_first,
        outer_sum(first_low, dinner),
        row_sum(dinner),
        outer_sum(active, douter),
        row_sum(douter),
        dgain_second,
        dshift_second,
    )
    return (tokens_grad, sums)


def per_device(
    tokens,
    doc_lengths,
    query_weight,
    query_bias,
    key_weight,
    value_weight,
    value_bias,
    out_weight,
    out_bias,
    first_gain,
    first_shift,
    inner_weight,
    inner_bias,
    outer_weight,
    outer_bias,
    second_gain,
    second_shift,
    cotangent,
):
    params = (
        query_weight,
        query_bias,
        key_weight,
        value_weight,
        value_bias,
        out_weight,
        out_bias,
        first_gain,
        first_shift,
        inner_weight,
        inner_bias,
        outer_weight,
        outer_bias,
        second_gain,
        second_shift,
    )
    rows = tokens.shape[2]
    base = lax.axis_index("ctx") * rows
    lengths = doc_lengths[:, 0]
    starts = jnp.cumsum(lengths, axis=-1) - lengths
    outputs = []
    token_parts = []
    sums = None
    for index in range(tokens.shape[0]):
        weights = (
            lax.all_gather(params[0], "wt", axis=0, tiled=True),
            lax.all_gather(params[1], "wt", axis=0, tiled=True),
            lax.all_gather(params[2], "wt", axis=0, tiled=True),
            lax.all_gather(params[3], "wt", axis=0, tiled=True),
            lax.all_gather(params[4], "wt", axis=0, tiled=True),
            lax.all_gather(params[5], "wt", axis=0, tiled=True),
            lax.all_gather(params[6], "wt", axis=0, tiled=True),
            lax.all_gather(params[7], "wt", axis=0, tiled=True),
            lax.all_gather(params[8], "wt", axis=0, tiled=True),
            lax.all_gather(params[9], "wt", axis=0, tiled=True),
            lax.all_gather(params[10], "wt", axis=0, tiled=True),
            lax.all_gather(params[11], "wt", axis=0, tiled=True),
            lax.all_gather(params[12], "wt", axis=0, tiled=True),
            lax.all_gather(params[13], "wt", axis=0, tiled=True),
            lax.all_gather(params[14], "wt", axis=0, tiled=True),
        )
        part_out, saved = forward_pass(
            tokens[index : index + 1, 0], starts[index : index + 1], weights, base
        )
        again = (
            lax.all_gather(params[0], "wt", axis=0, tiled=True),
            lax.all_gather(params[1], "wt", axis=0, tiled=True),
            lax.all_gather(params[2], "wt", axis=0, tiled=True),
            lax.all_gather(params[3], "wt", axis=0, tiled=True),
            lax.all_gather(params[4], "wt", axis=0, tiled=True),
            lax.all_gather(params[5], "wt", axis=0, tiled=True),
            lax.all_gather(params[6], "wt", axis=0, tiled=True),
            lax.all_gather(params[7], "wt", axis=0, tiled=True),
            lax.all_gather(params[8], "wt", axis=0, tiled=True),
            lax.all_gather(params[9], "wt", axis=0, tiled=True),
            lax.all_gather(params[10], "wt", axis=0, tiled=True),
            lax.all_gather(params[11], "wt", axis=0, tiled=True),
            lax.all_gather(params[12], "wt", axis=0, tiled=True),
            lax.all_gather(params[13], "wt", axis=0, tiled=True),
            lax.all_gather(params[14], "wt", axis=0, tiled=True),
        )
        part_grad, part_sums = backward_pass(
            saved, starts[index : index + 1], again, cotangent[index : index + 1, 0]
        )
        outputs.append(part_out)
        token_parts.append(part_grad)
        sums = part_sums if sums is None else jax.tree.map(jnp.add, sums, part_sums)
    output = jnp.concatenate(outputs, axis=0)
    tokens_grad = jnp.concatenate(token_parts, axis=0)
    shards = jax.tree.map(
        lambda part: part.astype(jnp.float32),
        lax.psum_scatter(for_sending(sums), "wt", scatter_dimension=0, tiled=True),
    )
    totals = lax.psum(shards, "ctx")
    return (output[:, None], tokens_grad[:, None]) + tuple(totals)


def solution(mesh):
    placed = (
        P(None, "wt", "ctx", None),
        P(None, "wt", None),
        P("wt", None),
        P("wt"),
        P("wt", None),
        P("wt", None),
        P("wt"),
        P("wt", None),
        P("wt"),
        P("wt"),
        P("wt"),
        P("wt", None),
        P("wt"),
        P("wt", None),
        P("wt"),
        P("wt"),
        P("wt"),
        P(None, "wt", "ctx", None),
    )
    return jax.shard_map(
        per_device,
        mesh=mesh,
        in_specs=placed,
        out_specs=(
            P(None, "wt", "ctx", None),
            P(None, "wt", "ctx", None),
            P("wt", None),
            P("wt"),
            P("wt", None),
            P("wt", None),
            P("wt"),
            P("wt", None),
            P("wt"),
            P("wt"),
            P("wt"),
            P("wt", None),
            P("wt"),
            P("wt", None),
            P("wt"),
            P("wt"),
            P("wt"),
        ),
        check_vma=False,
    )
```

profile of v0, /device:TPU:0, one launch (start us, length us, event | category | flops | bytes accessed | tf_op | source)
XLA Modules:
  0.0 1069.8 jit_solution(6935534509649645707)
XLA Ops:
  9.6 33.1 %all-gather.26.cloned.1.call-done = bf16[768,768]{1,0:T(8,128)(2,1)} async-done(((bf16[192,768]{1,0:T(8,128)(2,1)}), bf16[768,768]{1,0:T(8,128)(2,1)}) %all-gather.26.cloned.1.call-update) | async-done | bytes 1179664 | tf_op jit(solution)/shard_map/all_gather | solution.py:450
  42.7 2.5 convolution_convert_fusion.3
  48.2 18.0 %all-reduce.19 = (bf16[768]{0:T(1024)(128)(2,1)S(1)}, bf16[768]{0:T(1024)(128)(2,1)S(1)}, bf16[768]{0:T(1024)(128)(2,1)S(1)}, bf16[768]{0:T(1024)(128)(2,1)S(1)}...) all-reduce(bf16[768]{0:T(1024)(128)(2,1)S(1)} %dynamic-update-slice, ...), channel_id=1, replica_groups=mesh['ctx'=8,'wt'=4] {'wt'}, use_global_device_ids=true, to_apply=%add | all-reduce | flops 5376 | bytes 21504
  66.1 8.1 all-gather.30.cloned.1.call-done
  80.8 24.4 %all-gather.28.cloned.1.call-done = bf16[768,768]{1,0:T(8,128)(2,1)} async-done(((bf16[192,768]{1,0:T(8,128)(2,1)}), bf16[768,768]{1,0:T(8,128)(2,1)}) %all-gather.28.cloned.1.call-update) | async-done | bytes 1179664 | tf_op jit(solution)/shard_map/all_gather | solution.py:448
  108.3 13.1 %all-gather.10 = bf16[4,1,768]{2,1,0:T(2,128)(2,1)S(1)} all-gather(bf16[1,1,768]{2,1,0:T(2,128)(2,1)S(1)} %reshape.1961), channel_id=1, replica_groups=mesh['ctx'=8,'wt'=4] {'wt'}, dimensions={0}, use_global_device_ids=true | all-gather | bytes 7680 | tf_op jit(solution)/shard_map/all_gather | solution.py:458
  128.3 3.5 all-gather.38.cloned.1.call-done
  131.8 2.6 copy.127
  134.4 24.8 %all-gather.40.cloned.1.call-done = bf16[1024,768]{1,0:T(8,128)(2,1)} async-done(((bf16[128,768]{1,0:T(8,128)(2,1)}), bf16[1024,768]{1,0:T(8,128)(2,1)}) %all-gather.40.cloned.1.call-update) | async-done | bytes 1572880 | tf_op jit(solution)/shard_map/all_gather | solution.py:135
  159.1 2.6 copy.128
  161.7 17.7 %while.90 = (s32[]{:T(128)}, f32[1,12,128]{2,1,0:T(8,128)S(1)}, f32[1,12,128]{2,1,0:T(8,128)S(1)}, f32[1,128,12,64]{1,3,2,0:T(8,128)S(1)}, s32[1,16]{1,0:T(1,128...) while((s32[]{:T(128)}, f32[1,12,128]{2,1,0:T(8,128)S(1)}, ...), condition=%wide.region_8.9_spmd, body=%wide.region_2.8_spmd.sunk | while | flops 211842048 | bytes 15512505 | solution.py:67
  167.7 5.8 conditional.12
  179.5 11.3 %all-gather.32.cloned.1.call-done = bf16[768,768]{1,0:T(8,128)(2,1)} async-done(((bf16[192,768]{1,0:T(8,128)(2,1)}), bf16[768,768]{1,0:T(8,128)(2,1)}) %all-gather.32.cloned.1.call-update) | async-done | bytes 1179664 | tf_op jit(solution)/shard_map/all_gather | solution.py:453
  194.0 23.5 %all-gather.42.cloned.1.call-done = bf16[1024,768]{1,0:T(8,128)(2,1)} async-done(((bf16[128,768]{1,0:T(8,128)(2,1)}), bf16[1024,768]{1,0:T(8,128)(2,1)}) %all-gather.42.cloned.1.call-update) | async-done | bytes 1572880 | tf_op jit(solution)/shard_map/all_gather | solution.py:134
  219.3 25.8 %all-gather.44.cloned.1.call-done = bf16[1024,768]{1,0:T(8,128)(2,1)} async-done(((bf16[128,768]{1,0:T(8,128)(2,1)}), bf16[1024,768]{1,0:T(8,128)(2,1)}) %all-gather.44.cloned.1.call-update) | async-done | bytes 1572880 | tf_op jit(solution)/shard_map/all_gather | solution.py:135
  248.8 25.0 %while.91 = (s32[]{:T(128)}, f32[1,12,128]{2,1,0:T(8,128)S(1)}, f32[1,12,128]{2,1,0:T(8,128)}, f32[1,128,12,64]{1,3,2,0:T(8,128)}, s32[1,16]{1,0:T(1,128)}, /*in...) while((s32[]{:T(128)}, f32[1,12,128]{2,1,0:T(8,128)S(1)}, ...), condition=%wide.region_20.21_spmd, body=%wide.region_14.20_spmd.sunk | while | flops 211842048 | bytes 18969668 | solution.py:67
  255.2 6.0 conditional.13
  267.7 6.0 conditional.13
  279.1 56.9 %all-gather.34.cloned.1.call-done = bf16[768,3072]{1,0:T(8,128)(2,1)} async-done(((bf16[192,3072]{1,0:T(8,128)(2,1)}), bf16[768,3072]{1,0:T(8,128)(2,1)}) %all-gather.34.cloned.1.call-update) | async-done | bytes 4718608 | tf_op jit(solution)/shard_map/all_gather | solution.py:457
  336.0 4.5 convolution_add_fusion.1
  340.5 84.7 %all-gather.36.cloned.1.call-done = bf16[3072,768]{1,0:T(8,128)(2,1)} async-done(((bf16[768,768]{1,0:T(8,128)(2,1)}), bf16[3072,768]{1,0:T(8,128)(2,1)}) %all-gather.36.cloned.1.call-update) | async-done | bytes 4718608 | tf_op jit(solution)/shard_map/all_gather | solution.py:459
  425.3 4.0 fusion.203
  435.5 2.4 convert_reduce_fusion.7
  440.3 2.4 convert_reduce_fusion.6
  455.7 23.6 %while.92 = (s32[]{:T(128)}, f32[1,128,12,64]{1,3,2,0:T(8,128)}, s32[1,16]{1,0:T(1,128)}, s32[2]{0:T(128)}, s32[1,128]{1,0:T(1,128)}, /*index=5*/bf16[1,1024,768...) while((s32[]{:T(128)}, f32[1,128,12,64]{1,3,2,0:T(8,128)}, ...), condition=%wide.region_33.34_spmd, body=%wide.region_29.33_spmd.sunk | while | flops 307782144 | bytes 16278453 | solution.py:67
  462.6 10.0 conditional.14
  462.6 3.1 constant_dynamic-slice_fusion.4
  468.6 3.9 fusion.43
  485.9 27.8 %while.94 = (s32[]{:T(128)}, f32[1,128,12,64]{1,3,2,0:T(8,128)}, s32[1,16]{1,0:T(1,128)}, s32[2]{0:T(128)S(1)}, s32[1,128]{1,0:T(1,128)S(1)}, /*index=5*/bf16[1,...) while((s32[]{:T(128)}, f32[1,128,12,64]{1,3,2,0:T(8,128)}, ...), condition=%wide.region_47.48_spmd, body=%wide.region_43.0_spmd.sunk | while | flops 307782144 | bytes 16303057 | solution.py:67
  491.1 8.7 conditional.16
  491.1 3.1 constant_dynamic-slice_fusion.8
  495.9 3.9 fusion.82
  505.1 8.6 conditional.16
  505.1 3.0 constant_dynamic-slice_fusion.8
  509.7 3.9 fusion.82
  522.4 2.6 copy.138
  525.0 2.9 copy.146
  527.9 19.8 %all_gather.136 = f32[1,12,1024]{2,1,0:T(8,128)} all-gather(f32[1,12,128]{2,1,0:T(8,128)S(1)} %copy-done.101), channel_id=1, replica_groups=mesh['ctx'=8,'wt'=4] {'ctx'}, dimensions={2}, use_global_device_ids=true | all-gather | bytes 55296 | tf_op jit(solution)/shard_map/all_gather | solution.py:202
  547.7 9.1 all_gather.140
  556.8 10.0 all-gather.6
  566.7 9.8 all-gather.9
  578.6 3.0 copy.139
  581.6 2.8 copy.147
  586.0 37.0 %while.95 = (s32[]{:T(128)}, f32[1,128,12,64]{1,3,2,0:T(8,128)}, f32[1,128,12,64]{1,3,2,0:T(8,128)}, s32[1,16]{1,0:T(1,128)S(1)}, s32[2]{0:T(128)S(1)}, /*index=...) while((s32[]{:T(128)}, f32[1,128,12,64]{1,3,2,0:T(8,128)}, ...), condition=%wide.region_52.53_spmd, body=%wide.region_48.52_spmd.sunk | while | flops 412475904 | bytes 22402108 | solution.py:67
  590.5 14.1 %conditional.17 = ((f32[1,128,12,64]{1,3,2,0:T(8,128)}, f32[1,128,12,64]{1,3,2,0:T(8,128)})) conditional(s32[]{:T(128)} %bitcast.528, (f32[1,128,12,64]{1,3,2,0:T(8,128)}, f32[1,128,12,64]{1,3,2,0:T(8,128)}) %tuple.318, (s32[]{:T(128)}, bf16[1,1024,768]{1,2,0:T(8,128)(2,1)}, s32[1,512]{1,0:T(1,128)S(1)}, s32[1,128]{1,0:T(1,128)S(1)}, ...), branch_computations={%region_50.50_spmd, %region_51.51_spmd} | conditional | flops 412450816 | bytes 22391474 | solution.py:250
  590.5 3.2 constant_dynamic-slice_fusion.10
  596.7 4.7 fusion.103
  601.4 3.1 fusion.98
  609.0 13.9 %conditional.17 = ((f32[1,128,12,64]{1,3,2,0:T(8,128)}, f32[1,128,12,64]{1,3,2,0:T(8,128)})) conditional(s32[]{:T(128)} %bitcast.528, (f32[1,128,12,64]{1,3,2,0:T(8,128)}, f32[1,128,12,64]{1,3,2,0:T(8,128)}) %tuple.318, (s32[]{:T(128)}, bf16[1,1024,768]{1,2,0:T(8,128)(2,1)}, s32[1,512]{1,0:T(1,128)S(1)}, s32[1,128]{1,0:T(1,128)S(1)}, ...), branch_computations={%region_50.50_spmd, %region_51.51_spmd} | conditional | flops 412450816 | bytes 22391474 | solution.py:250
  609.1 3.0 constant_dynamic-slice_fusion.10
  615.1 4.7 fusion.103
  619.8 3.1 fusion.98
  626.2 26.6 %while.93 = (s32[]{:T(128)}, f32[1,128,12,64]{1,3,2,0:T(8,128)}, f32[1,128,12,64]{1,3,2,0:T(8,128)}, s32[1,16]{1,0:T(1,128)}, s32[2]{0:T(128)S(1)}, /*index=5*/s...) while((s32[]{:T(128)}, f32[1,128,12,64]{1,3,2,0:T(8,128)}, ...), condition=%wide.region_38.39_spmd, body=%wide.region_34.38_spmd.sunk | while | flops 412475904 | bytes 22402108 | solution.py:67
  632.2 14.7 %conditional.15 = ((f32[1,128,12,64]{1,3,2,0:T(8,128)}, f32[1,128,12,64]{1,3,2,0:T(8,128)})) conditional(s32[]{:T(128)} %bitcast.520, (f32[1,128,12,64]{1,3,2,0:T(8,128)}, f32[1,128,12,64]{1,3,2,0:T(8,128)}) %tuple.311, (s32[]{:T(128)}, bf16[1,1024,768]{1,2,0:T(8,128)(2,1)}, s32[1,512]{1,0:T(1,128)S(1)}, s32[1,128]{1,0:T(1,128)}, ...), branch_computations={%region_36.36_spmd, %region_37.37_spmd} | conditional | flops 412450816 | bytes 22391474 | solution.py:250
  632.2 3.1 constant_dynamic-slice_fusion.6
  639.1 4.7 fusion.64
  643.8 3.1 fusion.59
  663.9 3.7 add_convert_fusion.1
  670.5 3.2 add_convert_fusion
  687.0 17.7 %all-reduce.18 = (bf16[768]{0:T(1024)(128)(2,1)S(1)}, bf16[768]{0:T(1024)(128)(2,1)S(1)}, bf16[768]{0:T(1024)(128)(2,1)}, bf16[768]{0:T(1024)(128)(2,1)}, bf16[7...) all-reduce(bf16[768]{0:T(1024)(128)(2,1)} %copy-done.126, ...), channel_id=1, replica_groups=mesh['ctx'=8,'wt'=4] {'wt'}, use_global_device_ids=true, to_apply=%add.7 | all-reduce | flops 9984 | bytes 39936
  721.2 7.7 reduce-scatter.23.cloned.1.call-done
  730.0 85.7 %reduce-scatter.15.cloned.1.call-done = bf16[192,3072]{1,0:T(8,128)(2,1)} async-done(((bf16[768,3072]{1,0:T(8,128)(2,1)}), bf16[192,3072]{1,0:T(8,128)(2,1)}) %reduce-scatter.15.cloned.1.call-update) | async-done | bytes 1179664 | tf_op jit(solution)/shard_map/reduce_scatter | solution.py:494
  815.7 88.0 %reduce-scatter.17.cloned.1.call-done = bf16[768,768]{1,0:T(8,128)(2,1)} async-done(((bf16[3072,768]{1,0:T(8,128)(2,1)}), bf16[768,768]{1,0:T(8,128)(2,1)}) %reduce-scatter.17.cloned.1.call-update) | async-done | bytes 1179664 | tf_op jit(solution)/shard_map/reduce_scatter | solution.py:494
  903.7 155.8 %all-reduce.21 = (f32[192,768]{0,1:T(8,128)S(1)}, f32[192]{0:T(256)}, f32[192,768]{0,1:T(8,128)S(1)}, f32[192,768]{0,1:T(8,128)S(1)}, f32[192]{0:T(256)}, /*inde...) all-reduce(bf16[192,768]{0,1:T(8,128)(2,1)S(1)} %copy-done.71, ...), channel_id=1, replica_groups=mesh['ctx'=8,'wt'=4] {'ctx'}, use_global_device_ids=true, to_apply=%region_54.55 | all-reduce | flops 1771776 | bytes 10635264 | tf_op jit(solution)/shard_map/psum | solution.py:496
  (634 shorter events, 188.5 us)
Async XLA Ops:
  7.2 38.0 %copy-start.133 = (u32[32]{0:T(128)S(1)}, u32[32]{0:T(128)}, u32[]{:S(2)}) copy-start(u32[32]{0:T(128)} %constant.282) | copy-start | bytes 388
  7.2 67.0 %copy-start.15 = (bf16[2,1,128,768]{3,2,1,0:T(8,128)(2,1)S(1)}, bf16[2,1,128,768]{3,2,1,0:T(8,128)(2,1)}, u32[]{:S(2)}) copy-start(bf16[2,1,128,768]{3,2,1,0:T(8,128)(2,1)} %param.42) | copy-start | bytes 1179652
  7.2 39.3 %copy-start.143 = (bf16[192]{0:T(256)(128)(2,1)S(1)}, bf16[192]{0:T(256)(128)(2,1)}, u32[]{:S(2)}) copy-start(bf16[192]{0:T(256)(128)(2,1)} %param.45) | copy-start | bytes 1156
  7.2 39.5 %copy-start.144 = (bf16[192]{0:T(256)(128)(2,1)S(1)}, bf16[192]{0:T(256)(128)(2,1)}, u32[]{:S(2)}) copy-start(bf16[192]{0:T(256)(128)(2,1)} %param.48) | copy-start | bytes 1156
  7.2 39.8 %copy-start.145 = (bf16[192]{0:T(256)(128)(2,1)S(1)}, bf16[192]{0:T(256)(128)(2,1)}, u32[]{:S(2)}) copy-start(bf16[192]{0:T(256)(128)(2,1)} %param.50) | copy-start | bytes 1156
  7.2 40.0 %copy-start.146 = (bf16[192]{0:T(256)(128)(2,1)S(1)}, bf16[192]{0:T(256)(128)(2,1)}, u32[]{:S(2)}) copy-start(bf16[192]{0:T(256)(128)(2,1)} %param.56) | copy-start | bytes 1156
  7.3 40.2 %copy-start.147 = (bf16[192]{0:T(256)(128)(2,1)S(1)}, bf16[192]{0:T(256)(128)(2,1)}, u32[]{:S(2)}) copy-start(bf16[192]{0:T(256)(128)(2,1)} %param.52) | copy-start | bytes 1156
  7.3 40.4 %copy-start.148 = (bf16[192]{0:T(256)(128)(2,1)S(1)}, bf16[192]{0:T(256)(128)(2,1)}, u32[]{:S(2)}) copy-start(bf16[192]{0:T(256)(128)(2,1)} %param.51) | copy-start | bytes 1156
  7.3 40.7 %copy-start.149 = (bf16[192]{0:T(256)(128)(2,1)S(1)}, bf16[192]{0:T(256)(128)(2,1)}, u32[]{:S(2)}) copy-start(bf16[192]{0:T(256)(128)(2,1)} %param.57) | copy-start | bytes 1156
  7.3 35.4 %all-gather.26.cloned.1.call-start = ((), (), s32[]{:S(2)}) async-start(), calls=%async_computation.6 | async-start | bytes 1474560 | tf_op jit(solution)/shard_map/all_gather | solution.py:450
  8.0 66.2 %all-gather.30.cloned.1.call-start = ((), (), s32[]{:S(2)}) async-start(), calls=%async_computation.8 | async-start | bytes 1474560 | tf_op jit(solution)/shard_map/all_gather | solution.py:451
  8.8 96.5 %all-gather.28.cloned.1.call-start = ((), (), s32[]{:S(2)}) async-start(), calls=%async_computation.7 | async-start | bytes 1474560 | tf_op jit(solution)/shard_map/all_gather | solution.py:448
  9.5 122.3 %all-gather.38.cloned.1.call-start = ((), (), s32[]{:S(2)}) async-start(), calls=%async_computation.15 | async-start | bytes 1769472 | tf_op jit(solution)/shard_map/all_gather | solution.py:134
  42.7 34.6 %copy-start.18 = (bf16[768,768]{1,0:T(8,128)(2,1)S(1)}, bf16[768,768]{1,0:T(8,128)(2,1)}, u32[]{:S(2)}) copy-start(bf16[768,768]{1,0:T(8,128)(2,1)} %all-gather.26.cloned.1.call-done) | copy-start | bytes 3538948
  45.2 114.0 %all-gather.40.cloned.1.call-start = ((), (), s32[]{:S(2)}) async-start(), calls=%async_computation.16 | async-start | bytes 1769472 | tf_op jit(solution)/shard_map/all_gather | solution.py:135
  76.6 114.2 %all-gather.32.cloned.1.call-start = ((), (), s32[]{:S(2)}) async-start(), calls=%async_computation.9 | async-start | bytes 1474560 | tf_op jit(solution)/shard_map/all_gather | solution.py:453
  77.2 140.4 %all-gather.42.cloned.1.call-start = ((), (), s32[]{:S(2)}) async-start(), calls=%async_computation.17 | async-start | bytes 1769472 | tf_op jit(solution)/shard_map/all_gather | solution.py:134
  78.3 166.7 %all-gather.44.cloned.1.call-start = ((), (), s32[]{:S(2)}) async-start(), calls=%async_computation.18 | async-start | bytes 1769472 | tf_op jit(solution)/shard_map/all_gather | solution.py:135
  79.4 28.9 %copy-start.134 = (bf16[768]{0:T(1024)(128)(2,1)S(1)}, bf16[768]{0:T(1024)(128)(2,1)}, u32[]{:S(2)}) copy-start(bf16[768]{0:T(1024)(128)(2,1)} %param.54) | copy-start | bytes 4612
  79.4 42.7 %copy-start.132 = (s32[2,1,16]{2,1,0:T(1,128)S(1)}, s32[2,1,16]{2,1,0:T(1,128)}, u32[]{:S(2)}) copy-start(s32[2,1,16]{2,1,0:T(1,128)} %param.43) | copy-start | bytes 388
  79.4 256.6 %all-gather.34.cloned.1.call-start = ((), (), s32[]{:S(2)}) async-start(), calls=%async_computation.10 | async-start | bytes 5898240 | tf_op jit(solution)/shard_map/all_gather | solution.py:457
  80.1 345.1 %all-gather.36.cloned.1.call-start = ((), (), s32[]{:S(2)}) async-start(), calls=%async_computation.11 | async-start | bytes 5898240 | tf_op jit(solution)/shard_map/all_gather | solution.py:459
  80.7 441.6 %all-gather.46.cloned.1.call-start = ((), (), s32[]{:S(2)}) async-start(), calls=%async_computation.19 | async-start | bytes 1769472 | tf_op jit(solution)/shard_map/all_gather | solution.py:258
  105.2 21.5 %copy-start.22 = (bf16[768,768]{1,0:T(8,128)(2,1)S(1)}, bf16[768,768]{1,0:T(8,128)(2,1)}, u32[]{:S(2)}) copy-start(bf16[768,768]{1,0:T(8,128)(2,1)} %all-gather.28.cloned.1.call-done) | copy-start | bytes 3538948
  107.6 417.4 %all-gather.50.cloned.1.call-start = ((), (), s32[]{:S(2)}) async-start(), calls=%async_computation.21 | async-start | bytes 1769472 | tf_op jit(solution)/shard_map/all_gather | solution.py:258
  122.0 68.8 %copy-start.97 = (f32[768]{0:T(1024)}, f32[768]{0:T(1024)S(1)}, u32[]{:S(2)}) copy-start(f32[768]{0:T(1024)S(1)} %convert_element_type.642) | copy-start | bytes 9220
  127.8 450.8 %all-gather.48.cloned.1.call-start = ((), (), s32[]{:S(2)}) async-start(), calls=%async_computation.20 | async-start | bytes 1769472 | tf_op jit(solution)/shard_map/all_gather | solution.py:259
  179.4 38.1 %copy-start.38 = (f32[1,128,12,64]{1,3,2,0:T(8,128)}, f32[1,128,12,64]{1,3,2,0:T(8,128)S(1)}, u32[]{:S(2)}) copy-start(f32[1,128,12,64]{1,3,2,0:T(8,128)S(1)} %get-tuple-element.1089) | copy-start | bytes 1179652
  179.4 38.1 %copy-start.82 = (f32[1,12,128]{2,1,0:T(8,128)}, f32[1,12,128]{2,1,0:T(8,128)S(1)}, u32[]{:S(2)}) copy-start(f32[1,12,128]{2,1,0:T(8,128)S(1)} %get-tuple-element.1090) | copy-start | bytes 18436
  179.5 38.1 %copy-start.53 = (bf16[1,128,12,64]{1,3,2,0:T(8,128)(2,1)}, bf16[1,128,12,64]{1,3,2,0:T(8,128)(2,1)S(1)}, u32[]{:S(2)}) copy-start(bf16[1,128,12,64]{1,3,2,0:T(8,128)(2,1)S(1)} %fusion.160) | copy-start | bytes 589828
  192.6 54.2 %copy-start.104 = (f32[128]{0:T(128)}, f32[128]{0:T(128)S(1)}, u32[]{:S(2)}) copy-start(f32[128]{0:T(128)S(1)} %broadcast_multiply_fusion.3) | copy-start | bytes 1540
  193.5 53.3 %copy-start.139 = (f32[128]{0:T(128)}, f32[128]{0:T(128)S(1)}, u32[]{:S(2)}) copy-start(f32[128]{0:T(128)S(1)} %multiply_reduce_fusion.7) | copy-start | bytes 1540
  273.8 66.8 %copy-start.5 = (bf16[1,1024,768]{1,2,0:T(8,128)(2,1)}, bf16[1,1024,768]{1,2,0:T(8,128)(2,1)S(1)}, u32[]{:S(2)}) copy-start(bf16[1,1024,768]{1,2,0:T(8,128)(2,1)S(1)} %get-tuple-element.2480) | copy-start | bytes 4718596
  273.8 66.8 %copy-start.6 = (bf16[1,1024,768]{1,2,0:T(8,128)(2,1)}, bf16[1,1024,768]{1,2,0:T(8,128)(2,1)S(1)}, u32[]{:S(2)}) copy-start(bf16[1,1024,768]{1,2,0:T(8,128)(2,1)S(1)} %get-tuple-element.2481) | copy-start | bytes 4718596
  432.1 8.2 copy-start.26
  445.6 8.7 copy-start.34
  445.6 8.6 copy-start.36
  445.6 8.6 copy-start.135
  447.7 134.0 %all-gather.52.cloned.1.call-start = ((), (), s32[]{:S(2)}) async-start(), calls=%async_computation.22 | async-start | bytes 1769472 | tf_op jit(solution)/shard_map/all_gather | solution.py:259
  454.2 230.0 %reduce-scatter.19.cloned.1.call-start = ((), (), s32[]{:S(2)}) async-start(), calls=%async_computation.23 | async-start | bytes 1474560
  455.7 25.3 %copy-start.87 = (f32[1,12,128]{2,1,0:T(8,128)S(1)}, f32[1,12,128]{2,1,0:T(8,128)}, u32[]{:S(2)}) copy-start(f32[1,12,128]{2,1,0:T(8,128)} %get-tuple-element.1092) | copy-start | bytes 18436
  455.7 30.2 %copy-start.73 = (s32[1,128]{1,0:T(1,128)S(1)}, s32[1,128]{1,0:T(1,128)}, u32[]{:S(2)}) copy-start(s32[1,128]{1,0:T(1,128)} %get-tuple-element.2535) | copy-start | bytes 1540
  519.0 167.2 %reduce-scatter.13.cloned.1.call-start = ((), (), s32[]{:S(2)}) async-start(), calls=%async_computation.12 | async-start | bytes 1474560 | tf_op jit(solution)/shard_map/reduce_scatter | solution.py:494
  525.0 22.7 %copy-start.103 = (f32[1,12,128]{2,1,0:T(8,128)S(1)}, f32[1,12,128]{2,1,0:T(8,128)}, u32[]{:S(2)}) copy-start(f32[1,12,128]{2,1,0:T(8,128)} %get-tuple-element.2555) | copy-start | bytes 18436
  525.0 31.8 %copy-start.98 = (f32[1,12,128]{2,1,0:T(8,128)S(1)}, f32[1,12,128]{2,1,0:T(8,128)}, u32[]{:S(2)}) copy-start(f32[1,12,128]{2,1,0:T(8,128)} %get-tuple-element.2553) | copy-start | bytes 18436
  525.0 51.6 %copy-start.54 = (bf16[1,128,12,64]{1,3,2,0:T(8,128)(2,1)S(1)}, bf16[1,128,12,64]{1,3,2,0:T(8,128)(2,1)}, u32[]{:S(2)}) copy-start(bf16[1,128,12,64]{1,3,2,0:T(8,128)(2,1)} %copy-done.53) | copy-start | bytes 589828
  525.0 51.6 %copy-start.62 = (bf16[128,768]{1,0:T(8,128)(2,1)S(1)}, bf16[128,768]{1,0:T(8,128)(2,1)}, u32[]{:S(2)}) copy-start(bf16[128,768]{1,0:T(8,128)(2,1)} %copy-done.61) | copy-start | bytes 589828
  525.0 52.0 %copy-start.58 = (bf16[1,128,12,64]{1,3,2,0:T(8,128)(2,1)S(1)}, bf16[1,128,12,64]{1,3,2,0:T(8,128)(2,1)}, u32[]{:S(2)}) copy-start(bf16[1,128,12,64]{1,3,2,0:T(8,128)(2,1)} %copy-done.57) | copy-start | bytes 589828
  525.0 52.0 %copy-start.64 = (bf16[128,768]{1,0:T(8,128)(2,1)S(1)}, bf16[128,768]{1,0:T(8,128)(2,1)}, u32[]{:S(2)}) copy-start(bf16[128,768]{1,0:T(8,128)(2,1)} %copy-done.63) | copy-start | bytes 589828
  578.5 141.6 %reduce-scatter.21.cloned.1.call-start = ((), (), s32[]{:S(2)}) async-start(), calls=%async_computation.24 | async-start | bytes 1474560
  656.3 72.6 %reduce-scatter.23.cloned.1.call-start = ((), (), s32[]{:S(2)}) async-start(), calls=%async_computation.25 | async-start | bytes 1474560
  662.3 153.5 %reduce-scatter.15.cloned.1.call-start = ((), (), s32[]{:S(2)}) async-start(), calls=%async_computation.13 | async-start | bytes 5898240 | tf_op jit(solution)/shard_map/reduce_scatter | solution.py:494
  667.7 236.0 %reduce-scatter.17.cloned.1.call-start = ((), (), s32[]{:S(2)}) async-start(), calls=%async_computation.14 | async-start | bytes 5898240 | tf_op jit(solution)/shard_map/reduce_scatter | solution.py:494
  673.9 8.0 copy-start.35
  673.9 8.0 copy-start.136
  680.6 33.6 %copy-start.29 = (f32[128,768]{1,0:T(8,128)S(1)}, f32[128,768]{1,0:T(8,128)}, u32[]{:S(2)}) copy-start(f32[128,768]{1,0:T(8,128)} %copy-done.28) | copy-start | bytes 1179652
  680.6 33.6 %copy-start.31 = (f32[128,768]{1,0:T(8,128)S(1)}, f32[128,768]{1,0:T(8,128)}, u32[]{:S(2)}) copy-start(f32[128,768]{1,0:T(8,128)} %copy-done.30) | copy-start | bytes 1179652
  680.6 33.6 %copy-start.95 = (f32[768]{0:T(1024)S(1)}, f32[768]{0:T(1024)}, u32[]{:S(2)}) copy-start(f32[768]{0:T(1024)} %convert_element_type.649) | copy-start | bytes 9220
  681.9 34.0 %copy-start.19 = (bf16[768,768]{1,0:T(8,128)(2,1)S(1)}, bf16[768,768]{1,0:T(8,128)(2,1)}, u32[]{:S(2)}) copy-start(bf16[768,768]{1,0:T(8,128)(2,1)} %all-gather.26.cloned.1.call-done) | copy-start | bytes 3538948
  684.2 31.7 %copy-start.60 = (bf16[1,128,12,64]{1,3,2,0:T(8,128)(2,1)S(1)}, bf16[1,128,12,64]{1,3,2,0:T(8,128)(2,1)}, u32[]{:S(2)}) copy-start(bf16[1,128,12,64]{1,3,2,0:T(8,128)(2,1)} %convert_element_type.690) | copy-start | bytes 589828
  684.2 33.3 %copy-start.21 = (bf16[768,768]{1,0:T(8,128)(2,1)S(1)}, bf16[768,768]{1,0:T(8,128)(2,1)}, u32[]{:S(2)}) copy-start(bf16[768,768]{1,0:T(8,128)(2,1)} %all-gather.30.cloned.1.call-done) | copy-start | bytes 3538948
  684.2 33.3 %copy-start.70 = (bf16[1,128,12,64]{1,3,2,0:T(8,128)(2,1)S(1)}, bf16[1,128,12,64]{1,3,2,0:T(8,128)(2,1)}, u32[]{:S(2)}) copy-start(bf16[1,128,12,64]{1,3,2,0:T(8,128)(2,1)} %copy-done.69) | copy-start | bytes 589828
  718.6 185.1 %copy-start.71 = (bf16[192,768]{0,1:T(8,128)(2,1)S(1)}, bf16[192,768]{0,1:T(8,128)(2,1)}, u32[]{:S(2)}) copy-start(bf16[192,768]{0,1:T(8,128)(2,1)} %copy.174) | copy-start | bytes 884740
  718.6 185.1 %copy-start.131 = (f32[192]{0:T(256)S(1)}, f32[192]{0:T(256)}, u32[]{:S(2)}) copy-start(f32[192]{0:T(256)} %dynamic-slice_convert_fusion.6) | copy-start | bytes 2308
  (118 other events, 316.3 us)
Sparse Core Ops, SparseCore 0:
  9.7 32.9 all-gather.25
  44.2 29.9 all-gather.29
  75.8 29.3 all-gather.27
  107.0 24.7 all-gather.37
  133.5 25.5 all-gather.39
  160.5 30.2 all-gather.31
  192.7 24.7 all-gather.41
  219.4 25.5 all-gather.43
  246.6 89.3 all-gather.33
  337.5 87.7 all-gather.35
  427.2 23.9 all-gather.45
  452.9 25.5 all-gather.49
  480.4 25.5 all-gather.47
  507.8 25.6 all-gather.51
  535.6 29.3 reduce-scatter.18
  578.6 26.9 reduce-scatter.12
  656.5 41.9 reduce-scatter.20
  701.2 27.6 reduce-scatter.22
  731.2 84.5 reduce-scatter.14
  817.9 85.7 reduce-scatter.16
where the time goes:
time: 1080 us; the launch traced here: 1070 us
  waiting for transfers between devices  482 us (45%)
  blocking collectives  253 us (23%)
  local copies, waits for them, and re-layouts  113 us (10%)
  matrix products  102 us (9%)
  other arithmetic  61.2 us (6%)
  loops' own time  39.6 us (4%)
  between operations  18.3 us (2%)
    reduce_scatter x3, waiting for transfers between devices, per_device(): lax.psum_scatter(for_sending(sums), 'wt', scatter_dimension=0, tiled=True)  174 us
    psum x1, blocking collectives, per_device(): totals = lax.psum(shards, 'ctx')  156 us
    all_gather x1, waiting for transfers between devices, per_device(): lax.all_gather(params[11], 'wt', axis=0, tiled=True)  84.7 us
    all_gather x1, waiting for transfers between devices, per_device(): lax.all_gather(params[9], 'wt', axis=0, tiled=True)  56.9 us
    all_gather x2, waiting for transfers between devices, forward_attention(): lax.all_gather(values, 'ctx', axis=1, tiled=True)  50.5 us
    another operation x6, loops' own time, block_loop(): lax.scan(step, carry, jnp.arange(width // block, dtype=jnp.int32))  39 us
    unnamed x2, blocking collectives  35.6 us
    all_gather x1, waiting for transfers between devices, per_device(): lax.all_gather(params[2], 'wt', axis=0, tiled=True)  33.1 us
  transfers between devices with their start and end apart: 20, of which 13 were waited for; matrix products, arithmetic and copies ran while one was open for 24% of the time, Pallas kernels for 0%

commit v1 on v0

--- a/solution.py
+++ b/solution.py
@@ -3,6 +3,8 @@
 import jax
 import jax.numpy as jnp
 from jax import lax
+from jax.experimental import pallas as pl
+from jax.experimental.pallas import tpu as pltpu
 from jax.sharding import PartitionSpec as P
 
 HEADS = 12
@@ -399,7 +401,7 @@
     return (tokens_grad, sums)
 
 
-def per_device(
+def general_device(
     tokens,
     doc_lengths,
     query_weight,
@@ -497,6 +499,493 @@
     return (output[:, None], tokens_grad[:, None]) + tuple(totals)
 
 
+def flip(value, bits):
+    return lax.ppermute(value, "ctx", [(i, i ^ bits) for i in range(8)])
+
+
+def turn(value, step):
+    return lax.ppermute(value, "wt", [(i, (i - step) % 4) for i in range(4)])
+
+
+def pick(value, index, axis=0):
+    return lax.dynamic_index_in_dim(value, index, axis, keepdims=False)
+
+
+def pair(own, other, bit, axis=0):
+    return jnp.where(bit == 0, jnp.stack([own, other], axis), jnp.stack([other, own], axis))
+
+
+def place(shape, parts):
+    count = len(parts)
+
+    def kernel(*refs):
+        inputs, out, sems = refs[:count], refs[count], refs[count + 1]
+        ctx, own = lax.axis_index("ctx"), lax.axis_index("wt")
+        copies = []
+        for index, (unused, first, rows, start) in enumerate(parts):
+            at = pl.multiple_of(start(ctx, own), 16)
+            copies.append(
+                pltpu.make_async_copy(
+                    inputs[index].at[pl.ds(first, rows), :],
+                    out.at[pl.ds(at, rows), :],
+                    sems.at[index],
+                )
+            )
+        for copy in copies:
+            copy.start()
+        for copy in copies:
+            copy.wait()
+
+    return pl.pallas_call(
+        kernel,
+        out_shape=jax.ShapeDtypeStruct(shape, jnp.bfloat16),
+        in_specs=[pl.BlockSpec(memory_space=pl.ANY)] * count,
+        out_specs=pl.BlockSpec(memory_space=pl.ANY),
+        scratch_shapes=[pltpu.SemaphoreType.DMA((count,))],
+    )(*[part[0] for part in parts])
+
+
+def attend_kernel(near, far, weight, bias, seg_col, seg_row, qkv, mixed, logsum):
+    scale = HEAD_DIM ** (-0.5)
+    group = weight.shape[1] // (3 * HEAD_DIM)
+    half = near.shape[0]
+    block = 256
+    for index, source in enumerate((near, far)):
+
+        def project_rows(step, carry, index=index, source=source):
+            at = pl.multiple_of(step * block, block)
+            rows = source[pl.ds(at, block), :]
+            full = jnp.dot(rows, weight[...], preferred_element_type=jnp.float32) + bias[...]
+            low = full.astype(jnp.bfloat16)
+            for slot in range(3 * group):
+                qkv[slot, pl.ds(at + index * half, block), :] = low[
+                    :, slot * HEAD_DIM : (slot + 1) * HEAD_DIM
+                ]
+            return carry
+
+        lax.fori_loop(0, half // block, project_rows, 0)
+
+    def attend_rows(step, carry):
+        at = pl.multiple_of(step * block, block)
+        mask = seg_col[pl.ds(at, block), :] == seg_row[...]
+        sums = []
+        outs = []
+        for head in range(group):
+            query = qkv[head, pl.ds(at, block), :]
+            scores = lax.dot_general(
+                query,
+                qkv[group + head],
+                (((1,), (1,)), ((), ())),
+                preferred_element_type=jnp.float32,
+            )
+            scores = jnp.where(mask, scores * scale, NEG)
+            top = jnp.max(scores, axis=-1, keepdims=True)
+            expd = jnp.exp(scores - top)
+            total = jnp.sum(expd, axis=-1, keepdims=True)
+            probs = (expd * (1.0 / total)).astype(jnp.bfloat16)
+            out = jnp.dot(probs, qkv[2 * group + head], preferred_element_type=jnp.float32)
+            outs.append(out.astype(jnp.bfloat16))
+            sums.append(top + jnp.log(total))
+        mixed[pl.ds(at, block), :] = jnp.concatenate(outs, axis=1)
+        logsum[pl.ds(at, block), :] = jnp.concatenate(
+            sums + [jnp.zeros_like(sums[0])] * (128 - group), axis=1
+        )
+        return carry
+
+    lax.fori_loop(0, mixed.shape[0] // block, attend_rows, 0)
+
+
+def attend(near, far, weight, bias, seg):
+    rows = 2 * near.shape[0]
+    width = weight.shape[1] // 3
+    return pl.pallas_call(
+        attend_kernel,
+        out_shape=(
+            jax.ShapeDtypeStruct((3 * width // HEAD_DIM, rows, HEAD_DIM), jnp.bfloat16),
+            jax.ShapeDtypeStruct((rows, width), jnp.bfloat16),
+            jax.ShapeDtypeStruct((rows, 128), jnp.float32),
+        ),
+        compiler_params=pltpu.CompilerParams(vmem_limit_bytes=48 * 1024 * 1024),
+    )(near, far, weight, bias, seg[:, None], seg[None, :])
+
+
+def attend_back_kernel(
+    qkv, logsum, seg_col, seg_row, part0, part1, part2, part3, grads, dkeys, dvalues
+):
+    scale = HEAD_DIM ** (-0.5)
+    group = qkv.shape[0] // 3
+    width = group * HEAD_DIM
+    block = part0.shape[0]
+    dkeys[...] = jnp.zeros_like(dkeys)
+    dvalues[...] = jnp.zeros_like(dvalues)
+    for index, part in enumerate((part0, part1, part2, part3)):
+        at = index * block
+        mask = seg_col[at : at + block, :] == seg_row[...]
+        for head in range(group):
+            query = qkv[head, at : at + block, :]
+            grad = part[:, head * HEAD_DIM : (head + 1) * HEAD_DIM]
+            keys = qkv[group + head]
+            scores = lax.dot_general(
+                query, keys, (((1,), (1,)), ((), ())), preferred_element_type=jnp.float32
+            )
+            scores = jnp.where(mask, scores * scale, NEG)
+            probs = jnp.exp(scores - logsum[at : at + block, head : head + 1])
+            dprobs = lax.dot_general(
+                grad,
+                qkv[2 * group + head],
+                (((1,), (1,)), ((), ())),
+                preferred_element_type=jnp.float32,
+            )
+            delta = jnp.sum(probs * dprobs, axis=-1, keepdims=True)
+            dscores = (probs * (dprobs - delta)).astype(jnp.bfloat16)
+            dquery = jnp.dot(dscores, keys, preferred_element_type=jnp.float32) * scale
+            grads[at : at + block, head * HEAD_DIM : (head + 1) * HEAD_DIM] = dquery.astype(
+                jnp.bfloat16
+            )
+            dkeys[head] += lax.dot_general(
+                dscores, query, (((0,), (0,)), ((), ())), preferred_element_type=jnp.float32
+            )
+            dvalues[head] += lax.dot_general(
+                probs.astype(jnp.bfloat16),
+                grad,
+                (((0,), (0,)), ((), ())),
+                preferred_element_type=jnp.float32,
+            )
+    for head in range(group):
+        lanes = slice(width + head * HEAD_DIM, width + (head + 1) * HEAD_DIM)
+        grads[:, lanes] = (dkeys[head] * scale).astype(jnp.bfloat16)
+        lanes = slice(2 * width + head * HEAD_DIM, 2 * width + (head + 1) * HEAD_DIM)
+        grads[:, lanes] = dvalues[head].astype(jnp.bfloat16)
+
+
+def attend_back(qkv, logsum, seg, parts):
+    slots, rows, unused = qkv.shape
+    return pl.pallas_call(
+        attend_back_kernel,
+        out_shape=jax.ShapeDtypeStruct((rows, slots * HEAD_DIM), jnp.bfloat16),
+        scratch_shapes=[
+            pltpu.VMEM((slots // 3, rows, HEAD_DIM), jnp.float32),
+            pltpu.VMEM((slots // 3, rows, HEAD_DIM), jnp.float32),
+        ],
+        compiler_params=pltpu.CompilerParams(vmem_limit_bytes=48 * 1024 * 1024),
+    )(qkv, logsum, seg[:, None], seg[None, :], *parts)
+
+
+def dot(left, right):
+    return jnp.dot(left, right, preferred_element_type=jnp.float32)
+
+
+def dot_back(left, right):
+    return lax.dot_general(
+        left, right, (((1,), (1,)), ((), ())), preferred_element_type=jnp.float32
+    )
+
+
+def dot_sum(left, right):
+    return lax.dot_general(
+        left, right, (((0,), (0,)), ((), ())), preferred_element_type=jnp.float32
+    )
+
+
+def norm_parts(rows):
+    mean = jnp.mean(rows, axis=-1, keepdims=True)
+    centered = rows - mean
+    spread = jnp.mean(centered * centered, axis=-1, keepdims=True)
+    root = lax.rsqrt(spread + EPS)
+    return centered * root, root
+
+
+def norm_back(upstream, normed, root, gain):
+    grad = upstream * gain
+    mean = jnp.mean(grad, axis=-1, keepdims=True)
+    along = jnp.mean(grad * normed, axis=-1, keepdims=True)
+    return root * (grad - mean - normed * along)
+
+
+def short(value):
+    return value.astype(jnp.bfloat16)
+
+
+def wide(value):
+    return value.astype(jnp.float32)
+
+
+def add_sent(kept, received):
+    return short(wide(kept) + wide(received))
+
+
+def sum_owned(pieces, own):
+    total = wide(pick(pieces, own))
+    for step in (1, 2, 3):
+        total = total + wide(turn(pick(pieces, (own - step) % 4), step))
+    return short(total)
+
+
+def plane_device(
+    tokens,
+    doc_lengths,
+    query_weight,
+    query_bias,
+    key_weight,
+    value_weight,
+    value_bias,
+    out_weight,
+    out_bias,
+    first_gain,
+    first_shift,
+    inner_weight,
+    inner_bias,
+    outer_weight,
+    outer_bias,
+    second_gain,
+    second_shift,
+    cotangent,
+):
+    ctx, own = lax.axis_index("ctx"), lax.axis_index("wt")
+    core, x, y, group = ctx & 1, (ctx >> 1) & 1, ctx >> 2, ctx & 3
+    quarter = 2 * y + x
+    rows, dim = tokens.shape[2], tokens.shape[3]
+    shard = query_weight.shape[0]
+    hidden = outer_weight.shape[0]
+    half = hidden // 2
+    width = dim // 4
+
+    mine = jnp.concatenate([pick(tokens[:, 0], y), flip(pick(tokens[:, 0], 1 - y), 4)])
+    near = jnp.concatenate([mine, flip(mine, 2)])
+    far = flip(near, 1)
+
+    slices = [
+        lax.dynamic_slice_in_dim(w, group * width, width, 1)
+        for w in (query_weight, key_weight, value_weight)
+    ]
+    heads_own = jnp.concatenate(slices, axis=1)
+    heads_half = pick(heads_own.reshape(2, shard // 2, 3 * width), y)
+    parts = [(heads_own, 0, shard, lambda c, z: shard * z)]
+    for step in (1, 2, 3):
+        got = turn(heads_half, step)
+        parts.append(
+            (
+                got,
+                0,
+                shard // 2,
+                lambda c, z, s=step: shard * ((z + s) % 4) + (shard // 2) * (c >> 2),
+            )
+        )
+        parts.append(
+            (
+                flip(got, 4),
+                0,
+                shard // 2,
+                lambda c, z, s=step: shard * ((z + s) % 4) + (shard // 2) * (1 - (c >> 2)),
+            )
+        )
+    heads_weight = place((dim, 3 * width), parts)
+
+    packed = jnp.concatenate(
+        [
+            v.reshape(-1, shard)
+            for v in (
+                query_bias,
+                value_bias,
+                out_bias,
+                first_gain,
+                first_shift,
+                outer_bias,
+                second_gain,
+                second_shift,
+                inner_bias,
+            )
+        ]
+    )
+    rel = jnp.stack([packed] + [turn(packed, step) for step in (1, 2, 3)])
+    vectors = wide(lax.dynamic_slice_in_dim(jnp.concatenate([rel, rel]), (4 - own) % 4, 4))
+    rest = [vectors[:, i].reshape(dim) for i in range(2, 8)]
+    out_b, gain1, shift1, outer_b, gain2, shift2 = rest
+    mine_b = pick(vectors, group)
+    heads_bias = jnp.concatenate([mine_b[0], jnp.zeros_like(mine_b[0]), mine_b[1]])[None]
+    inner_b = pick(vectors[:, 8:].reshape(4, 2, half), core, 1).reshape(4 * half)
+
+    inner_half = pick(inner_weight.reshape(shard, 4, 2, half), core, 2).reshape(shard, 4 * half)
+    outer_half = lax.dynamic_slice_in_dim(outer_weight, core * half, half, 0)
+    out_send = pick(out_weight.reshape(4, shard // 4, dim), quarter)
+    inner_send = pick(inner_half.reshape(4, shard // 4, 4 * half), quarter)
+    outer_send = pick(outer_half.reshape(4, half // 4, dim), quarter)
+
+    def quarters(piece, size, at, first, second):
+        one = flip(piece, 2 * first)
+        two = flip(piece, 2 * second)
+        both = flip(one, 2 * second)
+        found = []
+        for value, bits in ((piece, 0), (one, first), (two, second), (both, first | second)):
+            found.append(
+                (value, 0, size, lambda c, z, b=bits: at(c, z) + size * (((c >> 1) & 3) ^ b))
+            )
+        return found
+
+    def spread(piece, whole, size, at, first, second):
+        found = [(whole, 0, 4 * size, lambda c, z: at(c, z))]
+        for step in (1, 2, 3):
+            found += quarters(
+                turn(piece, step), size, lambda c, z, s=step: at(c, (z + s) % 4), first, second
+            )
+        return found
+
+    out_parts = spread(
+        out_send, out_weight, shard // 4, lambda c, z: shard * (z ^ (c & 3)), 1, 2
+    )
+    inner_parts = spread(inner_send, inner_half, shard // 4, lambda c, z: shard * z, 2, 1)
+    outer_parts = spread(outer_send, outer_half, half // 4, lambda c, z: half * z, 1, 2)
+    out_full = place((dim, dim), out_parts)
+    inner_full = place((dim, 4 * half), inner_parts)
+    outer_full = place((4 * half, dim), outer_parts)
+
+    lengths = pick(doc_lengths[:, 0], y)
+    starts = jnp.cumsum(lengths) - lengths
+    index = jnp.arange(8 * rows, dtype=jnp.int32)
+    code = index // rows
+    code = (code >> 2) | (code & 2) | ((code & 1) << 2)
+    positions = (ctx ^ code) * rows + index % rows
+    seg = jnp.sum((starts[None, :] <= positions[:, None]).astype(jnp.int32), axis=-1) - 1
+
+    qkv, mixed, logsum = attend(near, far, heads_weight, heads_bias, seg)
+
+    def to_owner(value):
+        blocks = value.reshape(4, 2 * rows, width)
+        return [blocks[0]] + [flip(blocks[2 * (b & 1) + (b >> 1)], b) for b in (1, 2, 3)]
+
+    mixed_own = jnp.concatenate(to_owner(mixed), axis=1)
+    first_sum = wide(mine) + dot(mixed_own, out_full) + out_b
+    normed1, root1 = norm_parts(first_sum)
+    first = normed1 * gain1 + shift1
+    first_low = short(first)
+    first_both = jnp.concatenate([first_low, flip(first_low, 1)])
+    inner = dot(first_both, inner_full) + inner_b
+    active = short(gelu(inner))
+    second_part = dot(active, outer_full)
+    second_sum = (
+        first + outer_b + second_part[: 2 * rows] + flip(second_part[2 * rows :], 1)
+    )
+    normed2, root2 = norm_parts(second_sum)
+    output_own = short(normed2 * gain2 + shift2)
+    output = pair(output_own[:rows], flip(output_own[rows:], 4), y)
+
+    upstream = wide(
+        jnp.concatenate([pick(cotangent[:, 0], y), flip(pick(cotangent[:, 0], 1 - y), 4)])
+    )
+    dsecond = norm_back(upstream, normed2, root2, gain2)
+    douter = short(dsecond)
+    dgain2, dshift2 = jnp.sum(upstream * normed2, axis=0), jnp.sum(upstream, axis=0)
+    douter_b = jnp.sum(wide(douter), axis=0)
+    douter_both = jnp.concatenate([douter, flip(douter, 1)])
+    dactive = dot_back(douter_both, outer_full)
+    unused, gelu_back = jax.vjp(gelu, inner)
+    dinner = short(gelu_back(dactive)[0])
+    dfirst_part = dot_back(dinner, inner_full)
+    dfirst = dsecond + dfirst_part[: 2 * rows] + flip(dfirst_part[2 * rows :], 1)
+    dinner_w = short(dot_sum(first_both, dinner))
+    douter_w = short(dot_sum(active, douter_both))
+    dinner_b = jnp.sum(wide(dinner), axis=0)
+
+    dfirst_sum = norm_back(dfirst, normed1, root1, gain1)
+    dbranch = short(dfirst_sum)
+    dgain1, dshift1 = jnp.sum(dfirst * normed1, axis=0), jnp.sum(dfirst, axis=0)
+    dout_b = jnp.sum(wide(dbranch), axis=0)
+    dmixed_own = short(dot_back(dbranch, out_full))
+    dparts = [dmixed_own[:, b * width : (b + 1) * width] for b in range(4)]
+    dparts = [dparts[0]] + [flip(dparts[b], b) for b in (1, 2, 3)]
+    dqkv = attend_back(qkv, logsum, seg, [dparts[0], dparts[2], dparts[1], dparts[3]])
+
+    dout_w = short(dot_sum(mixed_own, dbranch)).reshape(4, shard, dim)
+    dout_w = jnp.where(
+        (group & 1) == 0, dout_w, dout_w.reshape(2, 2, shard, dim)[:, ::-1].reshape(dout_w.shape)
+    )
+    dout_w = jnp.where(
+        (group & 2) == 0, dout_w, dout_w.reshape(2, 2, shard, dim)[::-1].reshape(dout_w.shape)
+    )
+
+    dtokens = dot_back(dqkv, heads_weight)
+    dtokens = dtokens[: 4 * rows] + wide(flip(short(dtokens[4 * rows :]), 1))
+    dtokens = dtokens[: 2 * rows] + wide(flip(short(dtokens[2 * rows :]), 2)) + dfirst_sum
+    tokens_grad = pair(dtokens[:rows], wide(flip(short(dtokens[rows:]), 4)), y)
+
+    both = jnp.concatenate([near, far])
+    dheads = short(dot_sum(both, dqkv)).reshape(4, shard, 3 * width)
+    dheads = sum_owned(dheads, own)
+    dheads = add_sent(dheads, flip(dheads, 4))
+    dheads = pair(dheads, flip(dheads, 2), x)
+    dheads = pair(dheads, flip(dheads, 1), core)
+    dheads = wide(jnp.transpose(dheads.reshape(2, 2, shard, 3, width), (3, 2, 1, 0, 4)))
+    dheads = dheads.reshape(3, shard, dim)
+    dheads_b = jnp.sum(wide(dqkv), axis=0).reshape(3, width)
+    dheads_b = dheads_b + turn(dheads_b, 1) + turn(dheads_b, 2) + turn(dheads_b, 3)
+    dheads_b = dheads_b + flip(dheads_b, 4)
+    dheads_b = pair(dheads_b, flip(dheads_b, 2), x)
+    dheads_b = pair(dheads_b, flip(dheads_b, 1), core)
+    dheads_b = pick(jnp.transpose(dheads_b, (1, 0, 2, 3)).reshape(4, 3, width), own)
+
+    def shares(value, first, second):
+        part = value.reshape(4, 2, 2, -1, value.shape[-1])
+        bits = {1: x, 2: y}
+        axes = {1: 2, 2: 1}
+        at = axes[first]
+        part = add_sent(
+            pick(part, bits[first], at), flip(pick(part, 1 - bits[first], at), 2 * first)
+        )
+        part = add_sent(
+            pick(part, bits[second], 1), flip(pick(part, 1 - bits[second], 1), 2 * second)
+        )
+        return sum_owned(part, own)
+
+    def joined(piece, first, second):
+        bits = {1: x, 2: y}
+        piece = pair(piece, flip(piece, 2 * first), bits[first])
+        piece = pair(piece, flip(piece, 2 * second), bits[second])
+        if first == 2:
+            piece = jnp.swapaxes(piece, 0, 1)
+        return piece.reshape(-1, piece.shape[-1])
+
+    dinner_w = joined(shares(dinner_w, 1, 2), 1, 2)
+    dinner_w = pair(
+        dinner_w.reshape(shard, 4, half), flip(dinner_w, 1).reshape(shard, 4, half), core, 2
+    )
+    dinner_w = wide(dinner_w.reshape(shard, 8 * half))
+    douter_w = joined(shares(douter_w, 2, 1), 2, 1)
+    douter_w = wide(pair(douter_w, flip(douter_w, 1), core).reshape(hidden, dim))
+    dout_w = dout_w.reshape(dim, dim)
+    dout_w = add_sent(dout_w, flip(dout_w, 1))
+    dout_w = wide(joined(shares(dout_w, 1, 2), 1, 2))
+
+    sums = jnp.stack([dout_b, dgain1, dshift1, douter_b, dgain2, dshift2])
+    sums = sums + flip(sums, 1)
+    inner_sums = pair(dinner_b.reshape(4, half), flip(dinner_b.reshape(4, half), 1), core, 1)
+    sums = jnp.concatenate([sums, inner_sums.reshape(-1, dim)])
+    sums = sums + flip(sums, 2)
+    sums = sums + flip(sums, 4)
+    sums = sums + turn(sums, 1) + turn(sums, 2) + turn(sums, 3)
+    small = lax.dynamic_slice_in_dim(sums[:6], own * shard, shard, 1)
+    dinner_b = pick(sums[6:].reshape(4, hidden), own)
+
+    return (
+        output[:, None],
+        tokens_grad[:, None],
+        dheads[0],
+        dheads_b[0],
+        dheads[1],
+        dheads[2],
+        dheads_b[2],
+        dout_w,
+        small[0],
+        small[1],
+        small[2],
+        dinner_w,
+        dinner_b,
+        douter_w,
+        small[3],
+        small[4],
+        small[5],
+    )
+
+
 def solution(mesh):
     placed = (
         P(None, "wt", "ctx", None),
@@ -518,8 +1007,9 @@
         P("wt"),
         P(None, "wt", "ctx", None),
     )
+    fits = mesh.shape["ctx"] == 8 and mesh.shape["wt"] == 4
     return jax.shard_map(
-        per_device,
+        plane_device if fits else general_device,
         mesh=mesh,
         in_specs=placed,
         out_specs=(

time: 1080 us -> 631 us (0.58)
  waiting for transfers between devices: 482 us -> 107 us
  blocking collectives: 253 us -> 0 us
  Pallas kernels: 0 us -> 240 us
  starting transfers between devices: 1.45 us -> 112 us
  matrix products: 102 us -> 31.3 us
  loops' own time: 39.6 us -> 0 us
  local copies, waits for them, and re-layouts: 113 us -> 82.2 us
  between operations: 18.3 us -> 2.49 us
  other arithmetic: 61.2 us -> 46.1 us
    all_gather x14 -> x0, waiting for transfers between devices: 296 us -> none  [the longest x1 84.7 us: per_device(): lax.all_gather(params[11], 'wt', axis=0, tiled=True)]
    pallas_call x0 -> x6, Pallas kernels: none -> 240 us  [the longest x4 213 us: place(): pl.pallas_call(kernel, out_shape=jax.ShapeDtypeStruct(shape, jnp.bfloat16...]
    reduce_scatter x3 -> x0, waiting for transfers between devices: 174 us -> none  [per_device(): lax.psum_scatter(for_sending(sums), 'wt', scatter_dimension=0, tiled=True)]
    psum x1 -> x0, blocking collectives: 156 us -> none  [per_device(): totals = lax.psum(shards, 'ctx')]
    ppermute x0 -> x106, starting transfers between devices: none -> 112 us  [the longest x73 60.2 us: flip(): return lax.ppermute(value, 'ctx', [(i, i ^ bits) for i in range(8)])]
    ppermute x0 -> x106, waiting for transfers between devices: none -> 107 us  [the longest x73 69.1 us: flip(): return lax.ppermute(value, 'ctx', [(i, i ^ bits) for i in range(8)])]
    dot_general x57 -> x11, matrix products: 102 us -> 31.3 us  [the longest x4 13.7 us: dot_back(): lax.dot_general(left, right, (((1,), (1,)), ((), ())), preferred_element_...]
    all_gather x5 -> x0, blocking collectives: 61.7 us -> none  [the longest x2 28.9 us: key_gradient(): lax.all_gather(logsum, 'ctx', axis=2, tiled=True)]
  transfers between devices with their start and end apart: 20 -> 106, of which waited for: 13 -> 36; matrix products, arithmetic and copies ran while one was open for 24% -> 20% of each run, Pallas kernels for 0% -> 39%
where the time goes in v1:
time: 631 us; the launch traced here: 621 us
  Pallas kernels  240 us (38%)
  starting transfers between devices  112 us (18%)
  waiting for transfers between devices  107 us (17%)
  local copies, waits for them, and re-layouts  82.2 us (13%)
  other arithmetic  46.1 us (7%)
  matrix products  31.3 us (5%)
    pallas_call x4, Pallas kernels, place(): pl.pallas_call(kernel, out_shape=jax.ShapeDtypeStruct(shape, jnp.bfloat16...  213 us
    ppermute x73, waiting for transfers between devices, flip(): return lax.ppermute(value, 'ctx', [(i, i ^ bits) for i in range(8)])  69.1 us
    ppermute x73, starting transfers between devices, flip(): return lax.ppermute(value, 'ctx', [(i, i ^ bits) for i in range(8)])  60.2 us
    ppermute x33, starting transfers between devices, turn(): return lax.ppermute(value, 'wt', [(i, (i - step) % 4) for i in range(4)])  51.5 us
    ppermute x33, waiting for transfers between devices, turn(): return lax.ppermute(value, 'wt', [(i, (i - step) % 4) for i in range(4)])  38 us
    unnamed x178, local copies, waits for them, and re-layouts  14.4 us
    pallas_call x1, Pallas kernels, attend(): pl.pallas_call(attend_kernel, out_shape=(jax.ShapeDtypeStruct((3 * width...  14 us
    dot_general x4, matrix products, dot_back(): lax.dot_general(left, right, (((1,), (1,)), ((), ())), preferred_element_...  13.7 us
  transfers between devices with their start and end apart: 106, of which 36 were waited for; matrix products, arithmetic and copies ran while one was open for 20% of the time, Pallas kernels for 39%

profile of v1, /device:TPU:0, one launch (start us, length us, event | category | flops | bytes accessed | tf_op | source)
XLA Modules:
  0.0 621.2 jit_solution(10454336569643652228)
XLA Ops:
  6.8 5.1 collective-permute-start.9
  14.5 2.8 collective-permute-start.15
  20.7 3.3 reshape.793
  35.4 3.5 collective-permute-done
  41.2 6.1 collective-permute-done.1
  48.9 2.1 collective-permute-start.7
  53.6 2.8 collective-permute-done.7.refs_5_
  60.6 3.9 collective-permute-done.8.refs_6_
  65.8 31.0 %shard_map.305.weight = bf16[768,576]{1,0:T(8,128)(2,1)} custom-call(bf16[192,576]{1,0:T(8,128)(2,1)} %copy-done.28, bf16[96,576]{1,0:T(8,128)(2,1)} %copy-done.64, bf16[96,576]{1,0:T(8,128)(2,1)} %copy-done.67, bf16[96,576]{1,0:T(8,128)(2,1)} %copy-done.65, bf16[96,576]{1,0:T(8,128)(2,1)} %copy-done.68, bf16[96,576]{1,0:T(8,128)(2,1)} %copy-done.66, ...), custom_call_target="tpu_custom_call" | custom-call | tf_op jit(solution)/shard_map/pallas_call | solution.py:539
  100.2 14.0 %shard_map.306 = (bf16[9,1024,64]{2,1,0:T(8,128)(2,1)}, bf16[1024,192]{1,0:T(8,128)(2,1)S(1)}, f32[1024,128]{1,0:T(8,128)S(1)}) custom-call(bf16[512,768]{1,0:T(8,128)(2,1)S(1)} %pad_maximum_fusion.near, bf16[512,768]{1,0:T(8,128)(2,1)S(1)} %collective-permute-done.2.far, bf16[768,576]{1,0:T(8,128)(2,1)S(1)} %copy-done.2, ...), custom_call_target="tpu_custom_call" | custom-call | tf_op jit(solution)/shard_map/pallas_call | solution.py:601
  122.5 1.8 collective-permute-start.28
  124.6 37.0 %shard_map.307 = bf16[768,768]{1,0:T(8,128)(2,1)} custom-call(bf16[192,768]{1,0:T(8,128)(2,1)} %refs_0_.1, bf16[48,768]{1,0:T(8,128)(2,1)} %collective-permute-done.15.refs_1_, bf16[48,768]{1,0:T(8,128)(2,1)} %copy-done.73, bf16[48,768]{1,0:T(8,128)(2,1)} %copy-done.74, bf16[48,768]{1,0:T(8,128)(2,1)} %copy-done.77, ...), custom_call_target="tpu_custom_call" | custom-call | tf_op jit(solution)/shard_map/pallas_call | solution.py:539
  162.4 3.0 collective-permute-start.40
  166.4 2.0 fusion.84
  172.9 8.8 %collective-permute-done.44.refs_5_ = bf16[96,768]{1,0:T(8,128)(2,1)S(1)} collective-permute-done((bf16[96,768]{1,0:T(8,128)(2,1)}, bf16[96,768]{1,0:T(8,128)(2,1)S(1)}, u32[]{:S(2)}, u32[]{:S(2)}) %collective-permute-start.44) | collective-permute-done | bytes 147488 | tf_op jit(solution)/shard_map/ppermute | solution.py:507
  197.7 2.1 collective-permute-done.50.refs_11_
  200.6 2.4 collective-permute-done.43.refs_4_
  203.7 2.3 collective-permute-done.47.refs_8_
  209.9 72.7 %shard_map.309 = bf16[1536,768]{1,0:T(8,128)(2,1)} custom-call(bf16[384,768]{1,0:T(8,128)(2,1)} %copy-done.23, bf16[96,768]{1,0:T(8,128)(2,1)} %copy-done.43, bf16[96,768]{1,0:T(8,128)(2,1)} %copy-done.49, bf16[96,768]{1,0:T(8,128)(2,1)} %copy-done.50, bf16[96,768]{1,0:T(8,128)(2,1)} %copy-done.55, bf16[96,768]{1,0:T(8,128)(2,1)} %copy-done.45, ...), custom_call_target="tpu_custom_call" | custom-call | tf_op jit(solution)/shard_map/pallas_call | solution.py:539
  282.7 72.7 %shard_map.308 = bf16[768,1536]{1,0:T(8,128)(2,1)} custom-call(bf16[192,1536]{1,0:T(8,128)(2,1)} %bitcast.224, bf16[48,1536]{1,0:T(8,128)(2,1)} %copy-done.42, bf16[48,1536]{1,0:T(8,128)(2,1)} %copy-done.44, bf16[48,1536]{1,0:T(8,128)(2,1)} %copy-done.46, bf16[48,1536]{1,0:T(8,128)(2,1)} %collective-permute-done.31.refs_4_, ...), custom_call_target="tpu_custom_call" | custom-call | tf_op jit(solution)/shard_map/pallas_call | solution.py:539
  355.4 5.1 multiply_convert_fusion
  365.6 1.8 fusion.78
  367.7 3.9 collective-permute-done.54
  373.0 2.0 convert_reduce_fusion.3
  377.0 6.4 %convert_reduce_fusion = (f32[1536]{0:T(1024)S(1)}, bf16[512,1536]{1,0:T(8,128)(2,1)}) fusion(f32[512,1536]{1,0:T(8,128)} %get-tuple-element.93, bf16[1536,768]{1,0:T(8,128)(2,1)} %shard_map.309, bf16[256,768]{1,0:T(8,128)(2,1)} %collective-permute-done.55, bf16[256,768]{1,0:T(8,128)(2,1)} %get-tuple-element.38), kind=kOutput, calls=%fused_computation.3 | convolution fusion | flops 1221327360 | bytes 7870464 | tf_op jit(solution)/shard_map/dot_general | solution.py:679
  383.5 3.7 fusion.86
  388.2 2.4 convolution_convert_fusion.1
  393.7 2.7 convolution_convert_fusion
  398.9 3.1 multiply_reduce_fusion
  415.0 2.4 rev.7
  419.5 3.1 bitcast_select_fusion
  422.6 5.4 collective-permute-done.85
  429.5 2.7 collective-permute-done.86
  435.0 13.1 %shard_map.310 = bf16[1024,576]{1,0:T(8,128)(2,1)S(1)} custom-call(bf16[9,1024,64]{2,1,0:T(8,128)(2,1)S(1)} %copy-done.4, f32[1024,128]{1,0:T(8,128)S(1)} %get-tuple-element.22.logsum, s32[1024,1]{1,0:T(8,128)S(1)} %copy.131.seg_col, s32[1,1024]{1,0:T(1,128)S(1)} %bitcast.215, bf16[256,192]{1,0:T(8,128)(2,1)S(1)} %get-tuple-element.68.part0, ...), custom_call_target="tpu_custom_call" | custom-call | tf_op jit(solution)/shard_map/pallas_call | solution.py:663
  448.6 3.7 collective-permute-start.69
  452.3 3.2 fusion.10
  459.1 3.1 fusion.87
  464.6 2.5 slice.231
  468.4 2.9 collective-permute-start.87
  474.2 3.3 collective-permute-start.63
  480.3 1.8 maximum_select_fusion.8
  482.1 2.0 collective-permute-done.65
  484.1 9.5 %collective-permute-done.64 = bf16[192,576]{1,0:T(8,128)(2,1)S(1)} collective-permute-done((bf16[192,576]{1,0:T(8,128)(2,1)}, bf16[192,576]{1,0:T(8,128)(2,1)S(1)}, u32[]{:S(2)}, u32[]{:S(2)}) %collective-permute-start.64) | collective-permute-done | bytes 221216 | tf_op jit(solution)/shard_map/ppermute | solution.py:507
  494.4 1.7 fusion.1
  498.4 15.6 %collective-permute-done.66 = bf16[192,576]{1,0:T(8,128)(2,1)S(1)} collective-permute-done((bf16[192,576]{1,0:T(8,128)(2,1)S(1)}, bf16[192,576]{1,0:T(8,128)(2,1)S(1)}, u32[]{:S(2)}, u32[]{:S(2)}) %collective-permute-start.66) | collective-permute-done | bytes 221216 | tf_op jit(solution)/shard_map/ppermute | solution.py:503
  518.5 4.5 collective-permute-done.67
  524.2 1.8 slice_add_fusion
  529.9 1.6 collective-permute-done.99
  534.0 2.9 collective-permute-done.94
  536.9 3.9 collective-permute-start.102
  540.8 1.6 collective-permute-done.93
  542.8 5.2 collective-permute-start.100
  549.9 5.1 collective-permute-done.101
  566.0 2.2 copy.138
  568.2 2.7 squeeze.175
  572.1 2.7 squeeze.177
  575.4 1.6 squeeze.178
  588.8 4.4 collective-permute-done.62
  594.3 2.8 collective-permute-done.77
  597.6 3.0 collective-permute-start.79
  601.5 2.0 collective-permute-done.80
  607.9 1.7 bitcast_convert_fusion
  613.0 1.8 copy.149
  614.8 2.9 reshape.816
  (518 shorter events, 178.0 us)
Async XLA Ops:
  6.8 23.1 %collective-permute-start.9 = (bf16[12,192]{1,0:T(8,128)(2,1)S(1)}, bf16[12,192]{1,0:T(8,128)(2,1)}, u32[]{:S(2)}, u32[]{:S(2)}) collective-permute-start(bf16[12,192]{1,0:T(8,128)(2,1)S(1)} %concatenate.144), channel_id=1, source_target_pairs={{0,3},{1,0},{2,1},{3,2},{4,7},{5,4},{6,5},{7,6},{8,11},{9,8},{10,9... | collective-permute-start | bytes 13832 | tf_op jit(solution)/shard_map/ppermute | solution.py:507
  12.0 19.6 %collective-permute-start.10 = (bf16[12,192]{1,0:T(8,128)(2,1)S(1)}, bf16[12,192]{1,0:T(8,128)(2,1)}, u32[]{:S(2)}, u32[]{:S(2)}) collective-permute-start(bf16[12,192]{1,0:T(8,128)(2,1)S(1)} %concatenate.144), channel_id=1, source_target_pairs={{0,2},{1,3},{2,0},{3,1},{4,6},{5,7},{6,4},{7,5},{8,10},{9,11},{10,... | collective-permute-start | bytes 13832 | tf_op jit(solution)/shard_map/ppermute | solution.py:507
  12.0 21.3 %collective-permute-start.11 = (bf16[12,192]{1,0:T(8,128)(2,1)S(1)}, bf16[12,192]{1,0:T(8,128)(2,1)}, u32[]{:S(2)}, u32[]{:S(2)}) collective-permute-start(bf16[12,192]{1,0:T(8,128)(2,1)S(1)} %concatenate.144), channel_id=1, source_target_pairs={{0,1},{1,2},{2,3},{3,0},{4,5},{5,6},{6,7},{7,4},{8,9},{9,10},{10,1... | collective-permute-start | bytes 13832 | tf_op jit(solution)/shard_map/ppermute | solution.py:507
  14.5 34.4 %collective-permute-start.15 = (bf16[48,768]{1,0:T(8,128)(2,1)}, bf16[48,768]{1,0:T(8,128)(2,1)}, u32[]{:S(2)}, u32[]{:S(2)}) collective-permute-start(bf16[48,768]{1,0:T(8,128)(2,1)} %dynamic-slice_bitcast_fusion.23), channel_id=1, source_target_pairs={{0,3},{1,0},{2,1},{3,2},{4,7},{5,4},{6,5},{7,6},{8,11},{9,8},{10,9... | collective-permute-start | bytes 221192 | tf_op jit(solution)/shard_map/ppermute | solution.py:507
  17.3 35.7 %collective-permute-start.19 = (bf16[48,768]{1,0:T(8,128)(2,1)}, bf16[48,768]{1,0:T(8,128)(2,1)}, u32[]{:S(2)}, u32[]{:S(2)}) collective-permute-start(bf16[48,768]{1,0:T(8,128)(2,1)} %dynamic-slice_bitcast_fusion.23), channel_id=1, source_target_pairs={{0,2},{1,3},{2,0},{3,1},{4,6},{5,7},{6,4},{7,5},{8,10},{9,11},{10,... | collective-permute-start | bytes 221192 | tf_op jit(solution)/shard_map/ppermute | solution.py:507
  29.9 21.0 %collective-permute-start.3 = (bf16[96,576]{1,0:T(8,128)(2,1)S(1)}, bf16[96,576]{1,0:T(8,128)(2,1)S(1)}, u32[]{:S(2)}, u32[]{:S(2)}) collective-permute-start(bf16[96,576]{1,0:T(8,128)(2,1)S(1)} %dynamic-slice_bitcast_fusion.19), channel_id=1, source_target_pairs={{0,3},{1,0},{2,1},{3,2},{4,7},{5,4},{6,5},{7,6},{8,11},{9,8},{10,9... | collective-permute-start | bytes 331784 | tf_op jit(solution)/shard_map/ppermute | solution.py:507
  31.6 20.9 %collective-permute-start.5 = (bf16[96,576]{1,0:T(8,128)(2,1)S(1)}, bf16[96,576]{1,0:T(8,128)(2,1)S(1)}, u32[]{:S(2)}, u32[]{:S(2)}) collective-permute-start(bf16[96,576]{1,0:T(8,128)(2,1)S(1)} %dynamic-slice_bitcast_fusion.19), channel_id=1, source_target_pairs={{0,2},{1,3},{2,0},{3,1},{4,6},{5,7},{6,4},{7,5},{8,10},{9,11},{10,... | collective-permute-start | bytes 331784 | tf_op jit(solution)/shard_map/ppermute | solution.py:507
  47.4 51.0 %collective-permute-start.2 = (bf16[512,768]{1,0:T(8,128)(2,1)S(1)}, bf16[512,768]{1,0:T(8,128)(2,1)S(1)}, u32[]{:S(2)}, u32[]{:S(2)}) collective-permute-start(bf16[512,768]{1,0:T(8,128)(2,1)S(1)} %pad_maximum_fusion.near), channel_id=1, source_target_pairs={{0,4},{4,0},{8,12},{12,8},{16,20},{20,16},{24,28},{28,24},{1,5},{5... | collective-permute-start | bytes 2359304 | tf_op jit(solution)/shard_map/ppermute | solution.py:503
  53.0 43.8 %collective-permute-start.23 = (bf16[48,768]{1,0:T(8,128)(2,1)}, bf16[48,768]{1,0:T(8,128)(2,1)S(1)}, u32[]{:S(2)}, u32[]{:S(2)}) collective-permute-start(bf16[48,768]{1,0:T(8,128)(2,1)} %dynamic-slice_bitcast_fusion.23), channel_id=1, source_target_pairs={{0,1},{1,2},{2,3},{3,0},{4,5},{5,6},{6,7},{7,4},{8,9},{9,10},{10,1... | collective-permute-start | bytes 221192 | tf_op jit(solution)/shard_map/ppermute | solution.py:507
  56.4 57.8 %collective-permute-start.16 = (bf16[48,768]{1,0:T(8,128)(2,1)}, bf16[48,768]{1,0:T(8,128)(2,1)S(1)}, u32[]{:S(2)}, u32[]{:S(2)}) collective-permute-start(bf16[48,768]{1,0:T(8,128)(2,1)} %collective-permute-done.15.refs_1_), channel_id=1, source_target_pairs={{0,8},{4,12},{8,0},{12,4},{16,24},{20,28},{24,16},{28,20},{1,9},{5... | collective-permute-start | bytes 221192 | tf_op jit(solution)/shard_map/ppermute | solution.py:503
  57.9 57.0 %collective-permute-start.17 = (bf16[48,768]{1,0:T(8,128)(2,1)}, bf16[48,768]{1,0:T(8,128)(2,1)S(1)}, u32[]{:S(2)}, u32[]{:S(2)}) collective-permute-start(bf16[48,768]{1,0:T(8,128)(2,1)} %collective-permute-done.15.refs_1_), channel_id=1, source_target_pairs={{0,16},{4,20},{8,24},{12,28},{16,0},{20,4},{24,8},{28,12},{1,17},{... | collective-permute-start | bytes 221192 | tf_op jit(solution)/shard_map/ppermute | solution.py:503
  64.5 51.9 %collective-permute-start.20 = (bf16[48,768]{1,0:T(8,128)(2,1)}, bf16[48,768]{1,0:T(8,128)(2,1)}, u32[]{:S(2)}, u32[]{:S(2)}) collective-permute-start(bf16[48,768]{1,0:T(8,128)(2,1)} %collective-permute-done.19.refs_5_), channel_id=1, source_target_pairs={{0,8},{4,12},{8,0},{12,4},{16,24},{20,28},{24,16},{28,20},{1,9},{5... | collective-permute-start | bytes 221192 | tf_op jit(solution)/shard_map/ppermute | solution.py:503
  96.8 21.7 %collective-permute-start.21 = (bf16[48,768]{1,0:T(8,128)(2,1)}, bf16[48,768]{1,0:T(8,128)(2,1)S(1)}, u32[]{:S(2)}, u32[]{:S(2)}) collective-permute-start(bf16[48,768]{1,0:T(8,128)(2,1)} %collective-permute-done.19.refs_5_), channel_id=1, source_target_pairs={{0,16},{4,20},{8,24},{12,28},{16,0},{20,4},{24,8},{28,12},{1,17},{... | collective-permute-start | bytes 221192 | tf_op jit(solution)/shard_map/ppermute | solution.py:503
  98.4 18.7 %collective-permute-start.24 = (bf16[48,768]{1,0:T(8,128)(2,1)S(1)}, bf16[48,768]{1,0:T(8,128)(2,1)}, u32[]{:S(2)}, u32[]{:S(2)}) collective-permute-start(bf16[48,768]{1,0:T(8,128)(2,1)S(1)} %collective-permute-done.23.refs_9_), channel_id=1, source_target_pairs={{0,8},{4,12},{8,0},{12,4},{16,24},{20,28},{24,16},{28,20},{1,9},{5... | collective-permute-start | bytes 221192 | tf_op jit(solution)/shard_map/ppermute | solution.py:503
  119.1 42.4 %collective-permute-start.14 = (bf16[256,192]{1,0:T(8,128)(2,1)S(1)}, bf16[256,192]{1,0:T(8,128)(2,1)S(1)}, u32[]{:S(2)}, u32[]{:S(2)}) collective-permute-start(bf16[256,192]{1,0:T(8,128)(2,1)S(1)} %get-tuple-element.62), channel_id=1, source_target_pairs={{0,12},{4,8},{8,4},{12,0},{16,28},{20,24},{24,20},{28,16},{1,13},{... | collective-permute-start | bytes 294920 | tf_op jit(solution)/shard_map/ppermute | solution.py:503
  119.4 42.9 %collective-permute-start.13 = (bf16[256,192]{1,0:T(8,128)(2,1)S(1)}, bf16[256,192]{1,0:T(8,128)(2,1)S(1)}, u32[]{:S(2)}, u32[]{:S(2)}) collective-permute-start(bf16[256,192]{1,0:T(8,128)(2,1)S(1)} %get-tuple-element.63), channel_id=1, source_target_pairs={{0,8},{4,12},{8,0},{12,4},{16,24},{20,28},{24,16},{28,20},{1,9},{5... | collective-permute-start | bytes 294920 | tf_op jit(solution)/shard_map/ppermute | solution.py:503
  121.5 44.0 %collective-permute-start.12 = (bf16[256,192]{1,0:T(8,128)(2,1)S(1)}, bf16[256,192]{1,0:T(8,128)(2,1)S(1)}, u32[]{:S(2)}, u32[]{:S(2)}) collective-permute-start(bf16[256,192]{1,0:T(8,128)(2,1)S(1)} %get-tuple-element.64), channel_id=1, source_target_pairs={{0,4},{4,0},{8,12},{12,8},{16,20},{20,16},{24,28},{28,24},{1,5},{5... | collective-permute-start | bytes 294920 | tf_op jit(solution)/shard_map/ppermute | solution.py:503
  122.5 45.9 %collective-permute-start.28 = (bf16[48,1536]{1,0:T(8,128)(2,1)}, bf16[48,1536]{1,0:T(8,128)(2,1)S(1)}, u32[]{:S(2)}, u32[]{:S(2)}) collective-permute-start(bf16[48,1536]{1,0:T(8,128)(2,1)} %dynamic-slice_bitcast_fusion.18), channel_id=1, source_target_pairs={{0,3},{1,0},{2,1},{3,2},{4,7},{5,4},{6,5},{7,6},{8,11},{9,8},{10,9... | collective-permute-start | bytes 442376 | tf_op jit(solution)/shard_map/ppermute | solution.py:507
  124.3 45.1 %collective-permute-start.32 = (bf16[48,1536]{1,0:T(8,128)(2,1)}, bf16[48,1536]{1,0:T(8,128)(2,1)}, u32[]{:S(2)}, u32[]{:S(2)}) collective-permute-start(bf16[48,1536]{1,0:T(8,128)(2,1)} %dynamic-slice_bitcast_fusion.18), channel_id=1, source_target_pairs={{0,2},{1,3},{2,0},{3,1},{4,6},{5,7},{6,4},{7,5},{8,10},{9,11},{10,... | collective-permute-start | bytes 442376 | tf_op jit(solution)/shard_map/ppermute | solution.py:507
  165.4 16.3 %collective-permute-start.44 = (bf16[96,768]{1,0:T(8,128)(2,1)}, bf16[96,768]{1,0:T(8,128)(2,1)S(1)}, u32[]{:S(2)}, u32[]{:S(2)}) collective-permute-start(bf16[96,768]{1,0:T(8,128)(2,1)} %dynamic-slice_bitcast_fusion.17), channel_id=1, source_target_pairs={{0,2},{1,3},{2,0},{3,1},{4,6},{5,7},{6,4},{7,5},{8,10},{9,11},{10,... | collective-permute-start | bytes 442376 | tf_op jit(solution)/shard_map/ppermute | solution.py:507
  168.4 14.5 %collective-permute-start.48 = (bf16[96,768]{1,0:T(8,128)(2,1)}, bf16[96,768]{1,0:T(8,128)(2,1)S(1)}, u32[]{:S(2)}, u32[]{:S(2)}) collective-permute-start(bf16[96,768]{1,0:T(8,128)(2,1)} %dynamic-slice_bitcast_fusion.17), channel_id=1, source_target_pairs={{0,1},{1,2},{2,3},{3,0},{4,5},{5,6},{6,7},{7,4},{8,9},{9,10},{10,1... | collective-permute-start | bytes 442376 | tf_op jit(solution)/shard_map/ppermute | solution.py:507
  169.4 14.2 %collective-permute-start.29 = (bf16[48,1536]{1,0:T(8,128)(2,1)S(1)}, bf16[48,1536]{1,0:T(8,128)(2,1)S(1)}, u32[]{:S(2)}, u32[]{:S(2)}) collective-permute-start(bf16[48,1536]{1,0:T(8,128)(2,1)S(1)} %collective-permute-done.28.refs_1_), channel_id=1, source_target_pairs={{0,16},{4,20},{8,24},{12,28},{16,0},{20,4},{24,8},{28,12},{1,17},{... | collective-permute-start | bytes 442376 | tf_op jit(solution)/shard_map/ppermute | solution.py:503
  170.4 14.0 %collective-permute-start.30 = (bf16[48,1536]{1,0:T(8,128)(2,1)S(1)}, bf16[48,1536]{1,0:T(8,128)(2,1)S(1)}, u32[]{:S(2)}, u32[]{:S(2)}) collective-permute-start(bf16[48,1536]{1,0:T(8,128)(2,1)S(1)} %collective-permute-done.28.refs_1_), channel_id=1, source_target_pairs={{0,8},{4,12},{8,0},{12,4},{16,24},{20,28},{24,16},{28,20},{1,9},{5... | collective-permute-start | bytes 442376 | tf_op jit(solution)/shard_map/ppermute | solution.py:503
  171.8 14.0 %collective-permute-start.33 = (bf16[48,1536]{1,0:T(8,128)(2,1)}, bf16[48,1536]{1,0:T(8,128)(2,1)}, u32[]{:S(2)}, u32[]{:S(2)}) collective-permute-start(bf16[48,1536]{1,0:T(8,128)(2,1)} %collective-permute-done.32.refs_5_), channel_id=1, source_target_pairs={{0,16},{4,20},{8,24},{12,28},{16,0},{20,4},{24,8},{28,12},{1,17},{... | collective-permute-start | bytes 442376 | tf_op jit(solution)/shard_map/ppermute | solution.py:503
  191.8 163.6 %collective-permute-start.27 = (bf16[256,768]{1,0:T(8,128)(2,1)S(1)}, bf16[256,768]{1,0:T(8,128)(2,1)}, u32[]{:S(2)}, u32[]{:S(2)}) collective-permute-start(bf16[256,768]{1,0:T(8,128)(2,1)S(1)} %fusion.28), channel_id=1, source_target_pairs={{0,4},{4,0},{8,12},{12,8},{16,20},{20,16},{24,28},{28,24},{1,5},{5... | collective-permute-start | bytes 1179656 | tf_op jit(solution)/shard_map/ppermute | solution.py:503
  195.6 10.4 %collective-permute-start.47 = (bf16[96,768]{1,0:T(8,128)(2,1)S(1)}, bf16[96,768]{1,0:T(8,128)(2,1)S(1)}, u32[]{:S(2)}, u32[]{:S(2)}) collective-permute-start(bf16[96,768]{1,0:T(8,128)(2,1)S(1)} %collective-permute-done.45.refs_6_), channel_id=1, source_target_pairs={{0,16},{4,20},{8,24},{12,28},{16,0},{20,4},{24,8},{28,12},{1,17},{... | collective-permute-start | bytes 442376 | tf_op jit(solution)/shard_map/ppermute | solution.py:503
  197.1 10.4 %collective-permute-start.51 = (bf16[96,768]{1,0:T(8,128)(2,1)S(1)}, bf16[96,768]{1,0:T(8,128)(2,1)S(1)}, u32[]{:S(2)}, u32[]{:S(2)}) collective-permute-start(bf16[96,768]{1,0:T(8,128)(2,1)S(1)} %collective-permute-done.49.refs_10_), channel_id=1, source_target_pairs={{0,16},{4,20},{8,24},{12,28},{16,0},{20,4},{24,8},{28,12},{1,17},{... | collective-permute-start | bytes 442376 | tf_op jit(solution)/shard_map/ppermute | solution.py:503
  199.8 82.9 %collective-permute-start.38 = (bf16[48,1536]{1,0:T(8,128)(2,1)}, bf16[48,1536]{1,0:T(8,128)(2,1)}, u32[]{:S(2)}, u32[]{:S(2)}) collective-permute-start(bf16[48,1536]{1,0:T(8,128)(2,1)} %collective-permute-done.36.refs_9_), channel_id=1, source_target_pairs={{0,8},{4,12},{8,0},{12,4},{16,24},{20,28},{24,16},{28,20},{1,9},{5... | collective-permute-start | bytes 442376 | tf_op jit(solution)/shard_map/ppermute | solution.py:503
  202.9 79.7 %collective-permute-start.31 = (bf16[48,1536]{1,0:T(8,128)(2,1)S(1)}, bf16[48,1536]{1,0:T(8,128)(2,1)}, u32[]{:S(2)}, u32[]{:S(2)}) collective-permute-start(bf16[48,1536]{1,0:T(8,128)(2,1)S(1)} %collective-permute-done.29.refs_2_), channel_id=1, source_target_pairs={{0,8},{4,12},{8,0},{12,4},{16,24},{20,28},{24,16},{28,20},{1,9},{5... | collective-permute-start | bytes 442376 | tf_op jit(solution)/shard_map/ppermute | solution.py:503
  206.0 76.7 %collective-permute-start.35 = (bf16[48,1536]{1,0:T(8,128)(2,1)}, bf16[48,1536]{1,0:T(8,128)(2,1)}, u32[]{:S(2)}, u32[]{:S(2)}) collective-permute-start(bf16[48,1536]{1,0:T(8,128)(2,1)} %collective-permute-done.33.refs_6_), channel_id=1, source_target_pairs={{0,8},{4,12},{8,0},{12,4},{16,24},{20,28},{24,16},{28,20},{1,9},{5... | collective-permute-start | bytes 442376 | tf_op jit(solution)/shard_map/ppermute | solution.py:503
  207.5 75.1 %collective-permute-start.39 = (bf16[48,1536]{1,0:T(8,128)(2,1)}, bf16[48,1536]{1,0:T(8,128)(2,1)}, u32[]{:S(2)}, u32[]{:S(2)}) collective-permute-start(bf16[48,1536]{1,0:T(8,128)(2,1)} %collective-permute-done.37.refs_10_), channel_id=1, source_target_pairs={{0,8},{4,12},{8,0},{12,4},{16,24},{20,28},{24,16},{28,20},{1,9},{5... | collective-permute-start | bytes 442376 | tf_op jit(solution)/shard_map/ppermute | solution.py:503
  387.2 11.7 %collective-permute-start.56 = (f32[256,768]{1,0:T(8,128)S(1)}, f32[256,768]{1,0:T(8,128)S(1)}, u32[]{:S(2)}, u32[]{:S(2)}) collective-permute-start(f32[256,768]{1,0:T(8,128)S(1)} %slice.194), channel_id=1, source_target_pairs={{0,4},{4,0},{8,12},{12,8},{16,20},{20,16},{24,28},{28,24},{1,5},{5... | collective-permute-start | bytes 2359304 | tf_op jit(solution)/shard_map/ppermute | solution.py:503
  387.6 11.3 %collective-permute-start.84 = (f32[4,384]{1,0:T(4,128)S(1)}, f32[4,384]{1,0:T(4,128)S(1)}, u32[]{:S(2)}, u32[]{:S(2)}) collective-permute-start(f32[4,384]{1,0:T(4,128)S(1)} %reshape.803), channel_id=1, source_target_pairs={{0,4},{4,0},{8,12},{12,8},{16,20},{20,16},{24,28},{28,24},{1,5},{5... | collective-permute-start | bytes 18440 | tf_op jit(solution)/shard_map/ppermute | solution.py:503
  393.0 101.5 %collective-permute-start.90 = (bf16[4,2,48,1536]{3,2,0,1:T(8,128)(2,1)}, bf16[4,2,48,1536]{3,2,0,1:T(8,128)(2,1)}, u32[]{:S(2)}, u32[]{:S(2)}) collective-permute-start(bf16[4,2,48,1536]{3,2,0,1:T(8,128)(2,1)} %bitcast.212), channel_id=1, source_target_pairs={{0,8},{4,12},{8,0},{12,4},{16,24},{20,28},{24,16},{28,20},{1,9},{5... | collective-permute-start | bytes 3538952 | tf_op jit(solution)/shard_map/ppermute | solution.py:503
  404.7 28.8 %collective-permute-start.57 = (bf16[256,192]{1,0:T(8,128)(2,1)}, bf16[256,192]{1,0:T(8,128)(2,1)S(1)}, u32[]{:S(2)}, u32[]{:S(2)}) collective-permute-start(bf16[256,192]{1,0:T(8,128)(2,1)} %get-tuple-element.67), channel_id=1, source_target_pairs={{0,8},{4,12},{8,0},{12,4},{16,24},{20,28},{24,16},{28,20},{1,9},{5... | collective-permute-start | bytes 294920 | tf_op jit(solution)/shard_map/ppermute | solution.py:503
  405.9 27.5 %collective-permute-start.58 = (bf16[256,192]{1,0:T(8,128)(2,1)}, bf16[256,192]{1,0:T(8,128)(2,1)S(1)}, u32[]{:S(2)}, u32[]{:S(2)}) collective-permute-start(bf16[256,192]{1,0:T(8,128)(2,1)} %get-tuple-element.66), channel_id=1, source_target_pairs={{0,4},{4,0},{8,12},{12,8},{16,20},{20,16},{24,28},{28,24},{1,5},{5... | collective-permute-start | bytes 294920 | tf_op jit(solution)/shard_map/ppermute | solution.py:503
  405.9 27.5 %collective-permute-start.59 = (bf16[256,192]{1,0:T(8,128)(2,1)}, bf16[256,192]{1,0:T(8,128)(2,1)S(1)}, u32[]{:S(2)}, u32[]{:S(2)}) collective-permute-start(bf16[256,192]{1,0:T(8,128)(2,1)} %get-tuple-element.65), channel_id=1, source_target_pairs={{0,12},{4,8},{8,4},{12,0},{16,28},{20,24},{24,20},{28,16},{1,13},{... | collective-permute-start | bytes 294920 | tf_op jit(solution)/shard_map/ppermute | solution.py:503
  418.2 9.8 %collective-permute-start.85 = (f32[10,768]{1,0:T(8,128)S(1)}, f32[10,768]{1,0:T(8,128)S(1)}, u32[]{:S(2)}, u32[]{:S(2)}) collective-permute-start(f32[10,768]{1,0:T(8,128)S(1)} %pad_maximum_fusion.13), channel_id=1, source_target_pairs={{0,8},{4,12},{8,0},{12,4},{16,24},{20,28},{24,16},{28,20},{1,9},{5... | collective-permute-start | bytes 92168 | tf_op jit(solution)/shard_map/ppermute | solution.py:503
  432.2 47.5 %collective-permute-start.53 = (bf16[128,768]{1,0:T(8,128)(2,1)}, bf16[128,768]{1,0:T(8,128)(2,1)}, u32[]{:S(2)}, u32[]{:S(2)}) collective-permute-start(bf16[128,768]{1,0:T(8,128)(2,1)} %get-tuple-element.72), channel_id=1, source_target_pairs={{0,16},{4,20},{8,24},{12,28},{16,0},{20,4},{24,8},{28,12},{1,17},{... | collective-permute-start | bytes 589832 | tf_op jit(solution)/shard_map/ppermute | solution.py:503
  455.5 17.6 %collective-permute-start.89 = (f32[10,768]{1,0:T(8,128)}, f32[10,768]{1,0:T(8,128)}, u32[]{:S(2)}, u32[]{:S(2)}) collective-permute-start(f32[10,768]{1,0:T(8,128)} %add.412), channel_id=1, source_target_pairs={{0,1},{1,2},{2,3},{3,0},{4,5},{5,6},{6,7},{7,4},{8,9},{9,10},{10,1... | collective-permute-start | bytes 92168 | tf_op jit(solution)/shard_map/ppermute | solution.py:507
  456.1 17.1 %collective-permute-start.88 = (f32[10,768]{1,0:T(8,128)}, f32[10,768]{1,0:T(8,128)}, u32[]{:S(2)}, u32[]{:S(2)}) collective-permute-start(f32[10,768]{1,0:T(8,128)} %add.412), channel_id=1, source_target_pairs={{0,2},{1,3},{2,0},{3,1},{4,6},{5,7},{6,4},{7,5},{8,10},{9,11},{10,... | collective-permute-start | bytes 92168 | tf_op jit(solution)/shard_map/ppermute | solution.py:507
  473.2 10.9 %collective-permute-start.65 = (bf16[192,576]{1,0:T(8,128)(2,1)}, bf16[192,576]{1,0:T(8,128)(2,1)S(1)}, u32[]{:S(2)}, u32[]{:S(2)}) collective-permute-start(bf16[192,576]{1,0:T(8,128)(2,1)} %get-tuple-element.52), channel_id=1, source_target_pairs={{0,1},{1,2},{2,3},{3,0},{4,5},{5,6},{6,7},{7,4},{8,9},{9,10},{10,1... | collective-permute-start | bytes 663560 | tf_op jit(solution)/shard_map/ppermute | solution.py:507
  473.2 20.4 %collective-permute-start.64 = (bf16[192,576]{1,0:T(8,128)(2,1)}, bf16[192,576]{1,0:T(8,128)(2,1)S(1)}, u32[]{:S(2)}, u32[]{:S(2)}) collective-permute-start(bf16[192,576]{1,0:T(8,128)(2,1)} %get-tuple-element.53), channel_id=1, source_target_pairs={{0,2},{1,3},{2,0},{3,1},{4,6},{5,7},{6,4},{7,5},{8,10},{9,11},{10,... | collective-permute-start | bytes 663560 | tf_op jit(solution)/shard_map/ppermute | solution.py:507
  474.2 19.4 %collective-permute-start.63 = (bf16[192,576]{1,0:T(8,128)(2,1)}, bf16[192,576]{1,0:T(8,128)(2,1)S(1)}, u32[]{:S(2)}, u32[]{:S(2)}) collective-permute-start(bf16[192,576]{1,0:T(8,128)(2,1)} %get-tuple-element.51), channel_id=1, source_target_pairs={{0,3},{1,0},{2,1},{3,2},{4,7},{5,4},{6,5},{7,6},{8,11},{9,8},{10,9... | collective-permute-start | bytes 663560 | tf_op jit(solution)/shard_map/ppermute | solution.py:507
  479.6 35.7 %collective-permute-start.98 = (bf16[4,2,96,768]{3,2,0,1:T(8,128)(2,1)}, bf16[4,2,96,768]{3,2,0,1:T(8,128)(2,1)S(1)}, u32[]{:S(2)}, u32[]{:S(2)}) collective-permute-start(bf16[4,2,96,768]{3,2,0,1:T(8,128)(2,1)} %bitcast.233), channel_id=1, source_target_pairs={{0,16},{4,20},{8,24},{12,28},{16,0},{20,4},{24,8},{28,12},{1,17},{... | collective-permute-start | bytes 3538952 | tf_op jit(solution)/shard_map/ppermute | solution.py:503
  484.1 74.4 %collective-permute-start.75 = (bf16[768,768]{1,0:T(8,128)(2,1)S(1)}, bf16[768,768]{1,0:T(8,128)(2,1)}, u32[]{:S(2)}, u32[]{:S(2)}) collective-permute-start(bf16[768,768]{1,0:T(8,128)(2,1)S(1)} %copy-done.11), channel_id=1, source_target_pairs={{0,4},{4,0},{8,12},{12,8},{16,20},{20,16},{24,28},{28,24},{1,5},{5... | collective-permute-start | bytes 3538952 | tf_op jit(solution)/shard_map/ppermute | solution.py:503
  493.6 30.6 %collective-permute-start.60 = (bf16[512,768]{1,0:T(8,128)(2,1)}, bf16[512,768]{1,0:T(8,128)(2,1)}, u32[]{:S(2)}, u32[]{:S(2)}) collective-permute-start(bf16[512,768]{1,0:T(8,128)(2,1)} %slice.231), channel_id=1, source_target_pairs={{0,4},{4,0},{8,12},{12,8},{16,20},{20,16},{24,28},{28,24},{1,5},{5... | collective-permute-start | bytes 2359304 | tf_op jit(solution)/shard_map/ppermute | solution.py:503
  493.8 20.3 %collective-permute-start.66 = (bf16[192,576]{1,0:T(8,128)(2,1)S(1)}, bf16[192,576]{1,0:T(8,128)(2,1)S(1)}, u32[]{:S(2)}, u32[]{:S(2)}) collective-permute-start(bf16[192,576]{1,0:T(8,128)(2,1)S(1)} %fusion.33), channel_id=1, source_target_pairs={{0,16},{4,20},{8,24},{12,28},{16,0},{20,4},{24,8},{28,12},{1,17},{... | collective-permute-start | bytes 663560 | tf_op jit(solution)/shard_map/ppermute | solution.py:503
  497.0 29.9 %collective-permute-start.91 = (bf16[4,48,1536]{2,1,0:T(8,128)(2,1)}, bf16[4,48,1536]{2,1,0:T(8,128)(2,1)}, u32[]{:S(2)}, u32[]{:S(2)}) collective-permute-start(bf16[4,48,1536]{2,1,0:T(8,128)(2,1)} %dynamic-slice_bitcast_fusion.1), channel_id=1, source_target_pairs={{0,16},{4,20},{8,24},{12,28},{16,0},{20,4},{24,8},{28,12},{1,17},{... | collective-permute-start | bytes 1769480 | tf_op jit(solution)/shard_map/ppermute | solution.py:503
  517.5 14.0 %collective-permute-start.99 = (bf16[4,96,768]{2,1,0:T(8,128)(2,1)}, bf16[4,96,768]{2,1,0:T(8,128)(2,1)}, u32[]{:S(2)}, u32[]{:S(2)}) collective-permute-start(bf16[4,96,768]{2,1,0:T(8,128)(2,1)} %dynamic-slice_bitcast_fusion), channel_id=1, source_target_pairs={{0,8},{4,12},{8,0},{12,4},{16,24},{20,28},{24,16},{28,20},{1,9},{5... | collective-permute-start | bytes 1769480 | tf_op jit(solution)/shard_map/ppermute | solution.py:503
  523.9 39.3 %collective-permute-start.68 = (bf16[2,192,576]{2,1,0:T(8,128)(2,1)}, bf16[2,192,576]{2,1,0:T(8,128)(2,1)}, u32[]{:S(2)}, u32[]{:S(2)}) collective-permute-start(bf16[2,192,576]{2,1,0:T(8,128)(2,1)} %maximum_select_fusion.7), channel_id=1, source_target_pairs={{0,4},{4,0},{8,12},{12,8},{16,20},{20,16},{24,28},{28,24},{1,5},{5... | collective-permute-start | bytes 1327112 | tf_op jit(solution)/shard_map/ppermute | solution.py:503
  528.3 14.1 %collective-permute-start.93 = (bf16[48,1536]{1,0:T(8,128)(2,1)S(1)}, bf16[48,1536]{1,0:T(8,128)(2,1)S(1)}, u32[]{:S(2)}, u32[]{:S(2)}) collective-permute-start(bf16[48,1536]{1,0:T(8,128)(2,1)S(1)} %get-tuple-element.60), channel_id=1, source_target_pairs={{0,2},{1,3},{2,0},{3,1},{4,6},{5,7},{6,4},{7,5},{8,10},{9,11},{10,... | collective-permute-start | bytes 442376 | tf_op jit(solution)/shard_map/ppermute | solution.py:507
  531.5 11.4 %collective-permute-start.92 = (bf16[48,1536]{1,0:T(8,128)(2,1)S(1)}, bf16[48,1536]{1,0:T(8,128)(2,1)S(1)}, u32[]{:S(2)}, u32[]{:S(2)}) collective-permute-start(bf16[48,1536]{1,0:T(8,128)(2,1)S(1)} %get-tuple-element.58), channel_id=1, source_target_pairs={{0,3},{1,0},{2,1},{3,2},{4,7},{5,4},{6,5},{7,6},{8,11},{9,8},{10,9... | collective-permute-start | bytes 442376 | tf_op jit(solution)/shard_map/ppermute | solution.py:507
  536.9 11.9 %collective-permute-start.102 = (bf16[96,768]{1,0:T(8,128)(2,1)S(1)}, bf16[96,768]{1,0:T(8,128)(2,1)S(1)}, u32[]{:S(2)}, u32[]{:S(2)}) collective-permute-start(bf16[96,768]{1,0:T(8,128)(2,1)S(1)} %get-tuple-element.56), channel_id=1, source_target_pairs={{0,1},{1,2},{2,3},{3,0},{4,5},{5,6},{6,7},{7,4},{8,9},{9,10},{10,1... | collective-permute-start | bytes 442376 | tf_op jit(solution)/shard_map/ppermute | solution.py:507
  542.4 12.6 %collective-permute-start.101 = (bf16[96,768]{1,0:T(8,128)(2,1)S(1)}, bf16[96,768]{1,0:T(8,128)(2,1)S(1)}, u32[]{:S(2)}, u32[]{:S(2)}) collective-permute-start(bf16[96,768]{1,0:T(8,128)(2,1)S(1)} %get-tuple-element.57), channel_id=1, source_target_pairs={{0,2},{1,3},{2,0},{3,1},{4,6},{5,7},{6,4},{7,5},{8,10},{9,11},{10,... | collective-permute-start | bytes 442376 | tf_op jit(solution)/shard_map/ppermute | solution.py:507
  542.8 14.3 %collective-permute-start.100 = (bf16[96,768]{1,0:T(8,128)(2,1)S(1)}, bf16[96,768]{1,0:T(8,128)(2,1)S(1)}, u32[]{:S(2)}, u32[]{:S(2)}) collective-permute-start(bf16[96,768]{1,0:T(8,128)(2,1)S(1)} %get-tuple-element.55), channel_id=1, source_target_pairs={{0,3},{1,0},{2,1},{3,2},{4,7},{5,4},{6,5},{7,6},{8,11},{9,8},{10,9... | collective-permute-start | bytes 442376 | tf_op jit(solution)/shard_map/ppermute | solution.py:507
  548.7 35.3 %collective-permute-start.61 = (bf16[256,768]{1,0:T(8,128)(2,1)}, bf16[256,768]{1,0:T(8,128)(2,1)}, u32[]{:S(2)}, u32[]{:S(2)}) collective-permute-start(bf16[256,768]{1,0:T(8,128)(2,1)} %slice.232), channel_id=1, source_target_pairs={{0,8},{4,12},{8,0},{12,4},{16,24},{20,28},{24,16},{28,20},{1,9},{5... | collective-permute-start | bytes 1179656 | tf_op jit(solution)/shard_map/ppermute | solution.py:503
  555.0 22.0 %collective-permute-start.95 = (bf16[48,1536]{1,0:T(8,128)(2,1)}, bf16[48,1536]{1,0:T(8,128)(2,1)}, u32[]{:S(2)}, u32[]{:S(2)}) collective-permute-start(bf16[48,1536]{1,0:T(8,128)(2,1)} %fusion.40), channel_id=1, source_target_pairs={{0,8},{4,12},{8,0},{12,4},{16,24},{20,28},{24,16},{28,20},{1,9},{5... | collective-permute-start | bytes 442376 | tf_op jit(solution)/shard_map/ppermute | solution.py:503
  557.9 21.7 %collective-permute-start.103 = (bf16[96,768]{1,0:T(8,128)(2,1)}, bf16[96,768]{1,0:T(8,128)(2,1)}, u32[]{:S(2)}, u32[]{:S(2)}) collective-permute-start(bf16[96,768]{1,0:T(8,128)(2,1)} %fusion.37), channel_id=1, source_target_pairs={{0,16},{4,20},{8,24},{12,28},{16,0},{20,4},{24,8},{28,12},{1,17},{... | collective-permute-start | bytes 442376 | tf_op jit(solution)/shard_map/ppermute | solution.py:503
  561.9 24.1 %collective-permute-start.76 = (bf16[4,2,48,768]{3,2,1,0:T(8,128)(2,1)}, bf16[4,2,48,768]{3,2,1,0:T(8,128)(2,1)}, u32[]{:S(2)}, u32[]{:S(2)}) collective-permute-start(bf16[4,2,48,768]{3,2,1,0:T(8,128)(2,1)} %dynamic-slice_bitcast_fusion.2), channel_id=1, source_target_pairs={{0,8},{4,12},{8,0},{12,4},{16,24},{20,28},{24,16},{28,20},{1,9},{5... | collective-permute-start | bytes 1769480 | tf_op jit(solution)/shard_map/ppermute | solution.py:503
  578.2 22.9 %collective-permute-start.96 = (bf16[2,48,1536]{2,1,0:T(8,128)(2,1)S(1)}, bf16[2,48,1536]{2,1,0:T(8,128)(2,1)S(1)}, u32[]{:S(2)}, u32[]{:S(2)}) collective-permute-start(bf16[2,48,1536]{2,1,0:T(8,128)(2,1)S(1)} %maximum_select_fusion.11), channel_id=1, source_target_pairs={{0,16},{4,20},{8,24},{12,28},{16,0},{20,4},{24,8},{28,12},{1,17},{... | collective-permute-start | bytes 884744 | tf_op jit(solution)/shard_map/ppermute | solution.py:503
  580.8 13.3 %collective-permute-start.104 = (bf16[2,96,768]{2,1,0:T(8,128)(2,1)S(1)}, bf16[2,96,768]{2,1,0:T(8,128)(2,1)S(1)}, u32[]{:S(2)}, u32[]{:S(2)}) collective-permute-start(bf16[2,96,768]{2,1,0:T(8,128)(2,1)S(1)} %maximum_select_fusion.12), channel_id=1, source_target_pairs={{0,8},{4,12},{8,0},{12,4},{16,24},{20,28},{24,16},{28,20},{1,9},{5... | collective-permute-start | bytes 884744 | tf_op jit(solution)/shard_map/ppermute | solution.py:503
  587.3 9.8 %collective-permute-start.77 = (bf16[4,48,768]{2,1,0:T(8,128)(2,1)S(1)}, bf16[4,48,768]{2,1,0:T(8,128)(2,1)S(1)}, u32[]{:S(2)}, u32[]{:S(2)}) collective-permute-start(bf16[4,48,768]{2,1,0:T(8,128)(2,1)S(1)} %dynamic-slice_bitcast_fusion.3), channel_id=1, source_target_pairs={{0,16},{4,20},{8,24},{12,28},{16,0},{20,4},{24,8},{28,12},{1,17},{... | collective-permute-start | bytes 884744 | tf_op jit(solution)/shard_map/ppermute | solution.py:503
  594.2 12.2 %collective-permute-start.105 = (bf16[384,768]{1,0:T(8,128)(2,1)S(1)}, bf16[384,768]{1,0:T(8,128)(2,1)}, u32[]{:S(2)}, u32[]{:S(2)}) collective-permute-start(bf16[384,768]{1,0:T(8,128)(2,1)S(1)} %bitcast.227), channel_id=1, source_target_pairs={{0,4},{4,0},{8,12},{12,8},{16,20},{20,16},{24,28},{28,24},{1,5},{5... | collective-permute-start | bytes 1769480 | tf_op jit(solution)/shard_map/ppermute | solution.py:503
  (126 other events, 1825.5 us)
